TPU v7x, 32 devices: a whole 2x2x4 slice. The times are simulated.
32 devices in a mesh: img: 4 (over z), band: 8 (over y, x, core).
Axes of the slice: x: 2, y: 2, z: 4, core: 2. Of those that a mesh axis runs over, the one named last changes fastest.
Arguments:
- pixels: bfloat16 [4, 4, 1024, 192], P(None, 'img', 'band'), may hold values from -4 to 4
- valid: int32 [4, 4, 1024, 192], P(None, 'img', 'band'), may hold values from 0 to 1, as said below
- codes: int32 [4, 4, 1024], P(None, 'img', 'band'), may hold values from 0 to 8191
- image_kind: int32 [4, 4], P(None, 'img'), may hold values from 0 to 1
- w_wide: float32 [3584, 2, 512], P(('img', 'band')), may hold values from -0.25 to 0.25
- w_narrow: float32 [2560, 2, 512], P(('img', 'band')), may hold values from -0.25 to 0.25
- w_edge: float32 [512, 448], P(('img', 'band')), may hold values from -0.25 to 0.25
- codebook: float32 [8192, 32], P(('img', 'band')), may hold values from -5 to 5
- norms: float32 [10, 512], replicated, may hold values from 0.25 to 1.75
- bases: float32 [4, 512, 512], replicated, may hold values from -0.25 to 0.25
- basis_edge: float32 [448, 448], replicated, may hold values from -0.25 to 0.25
- m_wide: float32 [3584, 2, 512], P(('img', 'band')), may hold values from -2.3841858e-06 to 2.3841858e-06
- v_wide: float32 [3584, 2, 512], P(('img', 'band')), may hold values from 1.4731672e-13 to 5.8926686e-13
- m_narrow: float32 [2560, 2, 512], P(('img', 'band')), may hold values from -2.3841858e-06 to 2.3841858e-06
- v_narrow: float32 [2560, 2, 512], P(('img', 'band')), may hold values from 1.4731672e-13 to 5.8926686e-13
- m_edge: float32 [512, 448], P(('img', 'band')), may hold values from -2.3841858e-06 to 2.3841858e-06
- v_edge: float32 [512, 448], P(('img', 'band')), may hold values from 1.4731672e-13 to 5.8926686e-13
- m_code: float32 [8192, 32], P(('img', 'band')), may hold values from -5.9604645e-07 to 5.9604645e-07
- v_code: float32 [8192, 32], P(('img', 'band')), may hold values from 9.207295e-15 to 3.682918e-14
- m_norm: float32 [10, 512], replicated, may hold values from -6.67572e-06 to 6.67572e-06
- v_norm: float32 [10, 512], replicated, may hold values from 1.3258505e-12 to 5.303402e-12
Outputs:
- new_wide: float32 [3584, 2, 512], P(('img', 'band'))
- new_m_wide: float32 [3584, 2, 512], P(('img', 'band'))
- new_v_wide: float32 [3584, 2, 512], P(('img', 'band'))
- new_narrow: float32 [2560, 2, 512], P(('img', 'band'))
- new_m_narrow: float32 [2560, 2, 512], P(('img', 'band'))
- new_v_narrow: float32 [2560, 2, 512], P(('img', 'band'))
- new_edge: float32 [512, 448], P(('img', 'band'))
- new_m_edge: float32 [512, 448], P(('img', 'band'))
- new_v_edge: float32 [512, 448], P(('img', 'band'))
- new_codebook: float32 [8192, 32], P(('img', 'band'))
- new_m_code: float32 [8192, 32], P(('img', 'band'))
- new_v_code: float32 [8192, 32], P(('img', 'band'))
- new_norms: float32 [10, 512], replicated
- new_m_norm: float32 [10, 512], replicated
- new_v_norm: float32 [10, 512], replicated
- grad_norm: float32 [], replicated
- loss: float32 [], replicated
Inputs may be any that keep to these rules, and one draw needn't show every extreme that they name: `valid`: 1 where a pixel counts; rows hold more counted pixels towards their end. `image_kind`: 0: the row is one image of 1024 tokens; 1: the row is four images of 256 tokens in order.
All inputs are finite; a program needn't handle non-finite values.
Results may differ from a plain program's by a relative error of at most 0.00075.
The roundings to bfloat16 on the way count: a program that leaves them out, or rounds other values in their place, can miss the bound.
Values may be sent and summed in bfloat16 or wider, within the bound.
A program may use at most 512 MiB of HBM per device.

v0:
```python
import jax
import jax.numpy as jnp
from jax import lax
from jax.sharding import PartitionSpec as P

HEADS = 8
HDIM = 64


norm_eps = 1e-05
adam_eps = 1e-08
clip_level = 0.001
beta_first = 0.5
beta_second = 0.6
rate_matrix = 0.02
rate_vector = 0.3
weight_decay = 0.01
commitment = 0.25
masked_score = -1000000000.0
highest = lax.Precision.HIGHEST


def matmul_plain(first_op, second_op):
    return jnp.dot(first_op, second_op, preferred_element_type=jnp.float32)


def matmul_trans(first_op, second_op):
    return lax.dot_general(
        first_op, second_op, (((1,), (1,)), ((), ())), preferred_element_type=jnp.float32
    )


def matmul_outer(first_op, second_op):
    return lax.dot_general(
        first_op, second_op, (((0,), (0,)), ((), ())), preferred_element_type=jnp.float32
    )


def layer_norm(hidden, scale_gain, offset):
    centred = hidden - jnp.mean(hidden, axis=-1, keepdims=True)
    spread = jnp.mean(centred * centred, axis=-1, keepdims=True)
    return centred * lax.rsqrt(spread + norm_eps) * scale_gain + offset


def gelu_tanh(inputs):
    return (
        0.5
        * inputs
        * (1.0 + jnp.tanh(0.7978845608028654 * (inputs + 0.044715 * inputs * inputs * inputs)))
    )


def split_heads(matrix):
    return matrix.reshape(matrix.shape[0], HEADS, HDIM)


def head_scores(q_heads, k_heads, allowed):
    scores = jnp.einsum(
        "qhd,khd->hqk", q_heads, k_heads, preferred_element_type=jnp.float32
    ) * HDIM ** (-0.5)
    return jnp.where(allowed[None], scores, masked_score)


def attend(queries, key_rows, value_rows, allowed):
    scores = head_scores(split_heads(queries), split_heads(key_rows), allowed)
    score_peak = jnp.max(scores, axis=-1, keepdims=True)
    expo = jnp.exp(scores - score_peak)
    total = jnp.sum(expo, axis=-1, keepdims=True)
    softmaxed = (expo / total).astype(jnp.bfloat16)
    attended = jnp.einsum(
        "hqk,khd->qhd", softmaxed, split_heads(value_rows), preferred_element_type=jnp.float32
    )
    return (
        attended.reshape(queries.shape[0], -1).astype(jnp.bfloat16),
        score_peak + jnp.log(total),
    )


def attend_back(queries, key_rows, value_rows, allowed, log_total, grad_out):
    q_heads = split_heads(queries)
    k_heads = split_heads(key_rows)
    v_heads = split_heads(value_rows)
    g_heads = split_heads(grad_out)
    softmaxed = jnp.exp(head_scores(q_heads, k_heads, allowed) - log_total)
    grad_soft = jnp.einsum("qhd,khd->hqk", g_heads, v_heads, preferred_element_type=jnp.float32)
    row_dot = jnp.sum(softmaxed * grad_soft, axis=-1, keepdims=True)
    grad_scores = (softmaxed * (grad_soft - row_dot)).astype(jnp.bfloat16)
    scale = HDIM ** (-0.5)
    grad_q = (
        jnp.einsum("hqk,khd->qhd", grad_scores, k_heads, preferred_element_type=jnp.float32) * scale
    )
    grad_k = (
        jnp.einsum("hqk,qhd->khd", grad_scores, q_heads, preferred_element_type=jnp.float32) * scale
    )
    grad_v = jnp.einsum(
        "hqk,qhd->khd", softmaxed.astype(jnp.bfloat16), g_heads, preferred_element_type=jnp.float32
    )
    return (
        grad_q.reshape(queries.shape[0], -1),
        grad_k.reshape(key_rows.shape[0], -1),
        grad_v.reshape(key_rows.shape[0], -1),
        row_dot[..., 0],
    )


def block_forward(hidden, wide_rows, narrow_rows, gain_rows, allowed):
    model_width = hidden.shape[1]
    normed = layer_norm(hidden, gain_rows[0], gain_rows[1]).astype(jnp.bfloat16)
    projected = matmul_trans(normed, wide_rows[: 3 * model_width]).astype(jnp.bfloat16)
    keys_values = (
        lax.all_gather(projected[:, model_width : 2 * model_width], "band", axis=0, tiled=True),
        lax.all_gather(projected[:, 2 * model_width :], "band", axis=0, tiled=True),
    )
    attended, log_total = attend(
        projected[:, :model_width], keys_values[0], keys_values[1], allowed
    )
    middle = hidden + matmul_plain(attended, narrow_rows[:model_width])
    second = layer_norm(middle, gain_rows[2], gain_rows[3]).astype(jnp.bfloat16)
    upper_in = matmul_trans(second, wide_rows[3 * model_width :])
    active = gelu_tanh(upper_in).astype(jnp.bfloat16)
    result = middle + matmul_plain(active, narrow_rows[model_width:])
    return (
        result,
        (
            hidden,
            normed,
            projected,
            keys_values,
            attended,
            log_total,
            middle,
            second,
            upper_in,
            active,
        ),
    )


def block_backward(grad_out, wide_rows, narrow_rows, gain_rows, allowed, saved):
    (
        hidden,
        normed,
        projected,
        keys_values,
        attended,
        log_total,
        middle,
        second,
        upper_in,
        active,
    ) = saved
    model_width = hidden.shape[1]
    grad_y = grad_out.astype(jnp.bfloat16)
    grad_down = matmul_outer(active, grad_y)
    grad_active = matmul_trans(grad_y, narrow_rows[model_width:])
    grad_upper = jax.vjp(gelu_tanh, upper_in)[1](grad_active)[0].astype(jnp.bfloat16)
    grad_up = matmul_outer(grad_upper, second)
    _, second_back = jax.vjp(layer_norm, middle, gain_rows[2], gain_rows[3])
    grad_mid, gain_two, offset_two = second_back(
        matmul_plain(grad_upper, wide_rows[3 * model_width :])
    )
    grad_mid = grad_mid + grad_out
    grad_attn = grad_mid.astype(jnp.bfloat16)
    grad_outproj = matmul_outer(attended, grad_attn)
    grad_att = matmul_trans(grad_attn, narrow_rows[:model_width]).astype(jnp.bfloat16)
    queries = projected[:, :model_width]
    grad_q, grad_keys, grad_values, row_dot = attend_back(
        queries, keys_values[0], keys_values[1], allowed, log_total, grad_att
    )
    grad_k, grad_v = (
        lax.psum_scatter(grad_keys, "band", scatter_dimension=0, tiled=True),
        lax.psum_scatter(grad_values, "band", scatter_dimension=0, tiled=True),
    )
    grad_mixed = jnp.concatenate([grad_q, grad_k, grad_v], axis=1).astype(jnp.bfloat16)
    grad_qkv = matmul_outer(grad_mixed, normed)
    _, first_back = jax.vjp(layer_norm, hidden, gain_rows[0], gain_rows[1])
    grad_in, gain_one, offset_one = first_back(
        matmul_plain(grad_mixed, wide_rows[: 3 * model_width])
    )
    gain_grads = jnp.stack([gain_one, offset_one, gain_two, offset_two], axis=0)
    return (
        grad_in + grad_mid,
        jnp.concatenate([grad_qkv, grad_up], axis=0),
        jnp.concatenate([grad_outproj, grad_down], axis=0),
        gain_grads,
    )


def micro_step(gathered, norms, pixel_rows, valid_rows, code_rows, allowed, count, latent_total):
    wide_all, narrow_all, edge_all, book_all = gathered
    patch_size = pixel_rows.shape[1]
    code_width = book_all.shape[1]
    edge_in = edge_all[:, :patch_size]
    edge_pix = edge_all[:, patch_size : 2 * patch_size]
    edge_qin = edge_all[:, 2 * patch_size : 2 * patch_size + code_width]
    edge_qout = edge_all[:, 2 * patch_size + code_width :]
    start = matmul_trans(pixel_rows, edge_in)
    encoded, enc_saved = block_forward(start, wide_all[:, 0], narrow_all[:, 0], norms[0:4], allowed)
    encoded_low = encoded.astype(jnp.bfloat16)
    latent = matmul_plain(encoded_low, edge_qin)
    one_hot = (
        code_rows[:, None] == jnp.arange(book_all.shape[0], dtype=jnp.int32)[None, :]
    ).astype(jnp.bfloat16)
    chosen = matmul_plain(one_hot, book_all)
    chosen_low = chosen.astype(jnp.bfloat16)
    begin = matmul_trans(chosen_low, edge_qout)
    decoded, dec_saved = block_forward(begin, wide_all[:, 1], narrow_all[:, 1], norms[4:8], allowed)
    final = layer_norm(decoded, norms[8], norms[9]).astype(jnp.bfloat16)
    predict = matmul_plain(final, edge_pix)
    error = predict - pixel_rows.astype(jnp.float32)
    pixel_mask = valid_rows.astype(jnp.float32)
    gap = chosen - latent
    loss_part = (
        jnp.sum(pixel_mask * (error * error + jnp.abs(error))) / count
        + (1.0 + commitment) * jnp.sum(gap * gap) / latent_total
    )
    grad_pred = (pixel_mask * (2.0 * error + jnp.sign(error)) / count).astype(jnp.bfloat16)
    grad_pixw = matmul_outer(final, grad_pred)
    _, final_back = jax.vjp(layer_norm, decoded, norms[8], norms[9])
    grad_dec, gain_last, offset_last = final_back(matmul_trans(grad_pred, edge_pix))
    grad_begin, dec_wide, dec_narrow, dec_gains = block_backward(
        grad_dec, wide_all[:, 1], narrow_all[:, 1], norms[4:8], allowed, dec_saved
    )
    grad_begin_low = grad_begin.astype(jnp.bfloat16)
    grad_qout = matmul_outer(grad_begin_low, chosen_low)
    grad_latent = (
        matmul_plain(grad_begin_low, edge_qout) - 2.0 * commitment * gap / latent_total
    ).astype(jnp.bfloat16)
    grad_book = lax.dot_general(
        one_hot.astype(jnp.float32),
        2.0 * gap / latent_total,
        (((0,), (0,)), ((), ())),
        precision=highest,
    )
    grad_qin = matmul_outer(encoded_low, grad_latent)
    grad_start, enc_wide, enc_narrow, enc_gains = block_backward(
        matmul_trans(grad_latent, edge_qin),
        wide_all[:, 0],
        narrow_all[:, 0],
        norms[0:4],
        allowed,
        enc_saved,
    )
    grad_inw = matmul_outer(grad_start.astype(jnp.bfloat16), pixel_rows)
    grads = (
        jnp.stack([enc_wide, dec_wide], axis=1),
        jnp.stack([enc_narrow, dec_narrow], axis=1),
        jnp.concatenate([grad_inw, grad_pixw, grad_qin, grad_qout], axis=1),
        grad_book,
    )
    norm_grad = jnp.concatenate([enc_gains, dec_gains, gain_last[None], offset_last[None]], axis=0)
    return (grads, norm_grad, loss_part)


def moments(gradient, first_old, second_old):
    first_new = beta_first * first_old + (1.0 - beta_first) * gradient
    second_new = beta_second * second_old + (1.0 - beta_second) * gradient * gradient
    return (first_new, second_new, first_new / (jnp.sqrt(second_new) + adam_eps))


def rotated_update(weight, gradient, first_old, second_old, basis_stack):
    turned = jnp.einsum("rld,lde->rle", gradient, basis_stack, precision=highest)
    first_new, second_new, direction = moments(turned, first_old, second_old)
    turned_back = jnp.einsum("rle,lde->rld", direction, basis_stack, precision=highest)
    return (weight - rate_matrix * (turned_back + weight_decay * weight), first_new, second_new)


def plain_update(weight, gradient, first_old, second_old):
    first_new, second_new, direction = moments(gradient, first_old, second_old)
    return (weight - rate_vector * (direction + weight_decay * weight), first_new, second_new)


def body(
    pixels,
    valid,
    codes,
    image_kind,
    w_wide,
    w_narrow,
    w_edge,
    codebook,
    norms,
    bases,
    basis_edge,
    m_wide,
    v_wide,
    m_narrow,
    v_narrow,
    m_edge,
    v_edge,
    m_code,
    v_code,
    m_norm,
    v_norm,
):
    band_count = lax.axis_size("band")
    band_index = lax.axis_index("band")
    row_count = pixels.shape[2]
    length = row_count * band_count
    batch_count = pixels.shape[0]
    layer_count = w_wide.shape[1]
    latent_total = batch_count * lax.axis_size("img") * length * codebook.shape[1]
    shards = (
        w_wide.astype(jnp.bfloat16),
        w_narrow.astype(jnp.bfloat16),
        w_edge.astype(jnp.bfloat16),
        codebook.astype(jnp.bfloat16),
    )
    count = lax.psum(jnp.sum(valid.astype(jnp.float32)), ("img", "band"))
    positions = jnp.arange(length, dtype=jnp.int32)
    own_positions = band_index * row_count + jnp.arange(row_count, dtype=jnp.int32)
    grad_sum = None
    norm_sum = None
    loss_sum = None
    for batch_index in range(batch_count):
        gathered = (
            lax.all_gather(shards[0], ("img", "band"), axis=0, tiled=True),
            lax.all_gather(shards[1], ("img", "band"), axis=0, tiled=True),
            lax.all_gather(shards[2], ("img", "band"), axis=0, tiled=True),
            lax.all_gather(shards[3], ("img", "band"), axis=0, tiled=True),
        )
        span = jnp.where(image_kind[batch_index, 0] == 0, length, length // 4)
        allowed = (own_positions // span)[:, None] == (positions // span)[None, :]
        local_grads, norm_grad, loss_part = micro_step(
            gathered,
            norms,
            pixels[batch_index, 0],
            valid[batch_index, 0],
            codes[batch_index, 0],
            allowed,
            count,
            latent_total,
        )
        local_grads = (
            lax.psum_scatter(local_grads[0], ("img", "band"), scatter_dimension=0, tiled=True),
            lax.psum_scatter(local_grads[1], ("img", "band"), scatter_dimension=0, tiled=True),
            lax.psum_scatter(local_grads[2], ("img", "band"), scatter_dimension=0, tiled=True),
            lax.psum_scatter(local_grads[3], ("img", "band"), scatter_dimension=0, tiled=True),
        )
        if grad_sum is None:
            grad_sum, norm_sum, loss_sum = (local_grads, norm_grad, loss_part)
        else:
            grad_sum = jax.tree.map(jnp.add, grad_sum, local_grads)
            norm_sum = norm_sum + norm_grad
            loss_sum = loss_sum + loss_part
    squares = sum((jnp.sum(member * member) for member in grad_sum))
    norm_total, square_total, loss_total = lax.psum((norm_sum, squares, loss_sum), ("img", "band"))
    grad_norm = jnp.sqrt(square_total + jnp.sum(norm_total * norm_total))
    factor = jnp.minimum(1.0, clip_level / grad_norm)
    grad_wide, grad_narrow, grad_edge, grad_book = grad_sum
    new_wide, new_m_wide, new_v_wide = rotated_update(
        w_wide, factor * grad_wide, m_wide, v_wide, bases[:layer_count]
    )
    new_narrow, new_m_narrow, new_v_narrow = rotated_update(
        w_narrow, factor * grad_narrow, m_narrow, v_narrow, bases[layer_count:]
    )
    new_edge, new_m_edge, new_v_edge = rotated_update(
        w_edge[:, None],
        factor * grad_edge[:, None],
        m_edge[:, None],
        v_edge[:, None],
        basis_edge[None],
    )
    new_book, new_m_code, new_v_code = plain_update(codebook, factor * grad_book, m_code, v_code)
    new_norms, new_m_norm, new_v_norm = plain_update(norms, factor * norm_total, m_norm, v_norm)
    return (
        new_wide,
        new_m_wide,
        new_v_wide,
        new_narrow,
        new_m_narrow,
        new_v_narrow,
        new_edge[:, 0],
        new_m_edge[:, 0],
        new_v_edge[:, 0],
        new_book,
        new_m_code,
        new_v_code,
        new_norms,
        new_m_norm,
        new_v_norm,
        grad_norm,
        loss_total,
    )


def solution(mesh):
    in_specs = (
        P(None, "img", "band", None),
        P(None, "img", "band", None),
        P(None, "img", "band"),
        P(None, "img"),
        P(("img", "band"), None, None),
        P(("img", "band"), None, None),
        P(("img", "band"), None),
        P(("img", "band"), None),
        P(),
        P(),
        P(),
        P(("img", "band"), None, None),
        P(("img", "band"), None, None),
        P(("img", "band"), None, None),
        P(("img", "band"), None, None),
        P(("img", "band"), None),
        P(("img", "band"), None),
        P(("img", "band"), None),
        P(("img", "band"), None),
        P(),
        P(),
    )
    out_specs = (
        P(("img", "band"), None, None),
        P(("img", "band"), None, None),
        P(("img", "band"), None, None),
        P(("img", "band"), None, None),
        P(("img", "band"), None, None),
        P(("img", "band"), None, None),
        P(("img", "band"), None),
        P(("img", "band"), None),
        P(("img", "band"), None),
        P(("img", "band"), None),
        P(("img", "band"), None),
        P(("img", "band"), None),
        P(),
        P(),
        P(),
        P(),
        P(),
    )
    return jax.shard_map(body, mesh=mesh, in_specs=in_specs, out_specs=out_specs, check_vma=False)
```

profile of v0, /device:TPU:0, one launch (start us, length us, event | category | flops | bytes accessed | tf_op | source)
XLA Modules:
  0.0 1972.6 jit_solution(13376526611130125091)
XLA Ops:
  10.7 45.4 %all_gather.72 = bf16[512,448]{1,0:T(8,128)(2,1)S(1)} all-gather(bf16[16,448]{1,0:T(8,128)(2,1)S(1)} %convert_element_type.503), channel_id=1, replica_groups=mesh['img'=4,'band'=8] {'img','band'}, dimensions={0}, use_global_device_ids=true | all-gather | bytes 473088 | tf_op jit(solution)/shard_map/all_gather | solution.py:319
  56.9 39.2 %all_gather.77 = bf16[8192,32]{0,1:T(8,128)(2,1)S(1)} all-gather(bf16[256,32]{0,1:T(8,128)(2,1)S(1)} %convert_element_type.513), channel_id=1, replica_groups=mesh['img'=4,'band'=8] {'img','band'}, dimensions={0}, use_global_device_ids=true | all-gather | bytes 540672 | tf_op jit(solution)/shard_map/all_gather | solution.py:320
  136.3 37.6 %psum.28 = f32[]{:T(128)} all-reduce(f32[]{:T(128)} %convert_reduce_fusion), channel_id=1, replica_groups=mesh['img'=4,'band'=8] {'img','band'}, use_global_device_ids=true, to_apply=%region_15.16 | all-reduce | flops 1 | bytes 8 | tf_op jit(solution)/shard_map/psum | solution.py:309
  200.3 16.9 all-gather.25.cloned.1.call-done
  225.3 15.9 all-gather.35.cloned.1.call-done
  246.8 19.6 all-gather.37.cloned.1.call-done
  283.2 9.2 all-gather.27.cloned.1.call-done
  298.0 20.4 %all-gather.29.cloned.1.call-done = bf16[1024,512]{1,0:T(8,128)(2,1)} async-done(((bf16[128,512]{1,0:T(8,128)(2,1)}), bf16[1024,512]{1,0:T(8,128)(2,1)}) %all-gather.29.cloned.1.call-update) | async-done | bytes 1048592 | tf_op jit(solution)/shard_map/all_gather | solution.py:112
  334.7 9.6 all-gather.51.cloned.1.call-done
  351.3 18.9 all-gather.53.cloned.1.call-done
  485.8 11.1 all-gather.33.cloned.1.call-done
  499.1 23.0 %all-gather.49.cloned.1.call-done = bf16[1024,512]{1,0:T(8,128)(2,1)} async-done(((bf16[128,512]{1,0:T(8,128)(2,1)}), bf16[1024,512]{1,0:T(8,128)(2,1)}) %all-gather.49.cloned.1.call-update) | async-done | bytes 1048592 | tf_op jit(solution)/shard_map/all_gather | solution.py:112
  549.7 23.0 %all-gather.41.cloned.1.call-done = bf16[1024,512]{1,0:T(8,128)(2,1)} async-done(((bf16[128,512]{1,0:T(8,128)(2,1)}), bf16[1024,512]{1,0:T(8,128)(2,1)}) %all-gather.41.cloned.1.call-update) | async-done | bytes 1048592 | tf_op jit(solution)/shard_map/all_gather | solution.py:112
  632.8 29.3 %reduce-scatter.49.cloned.1.call-done = f32[128,512]{0,1:T(8,128)} async-done(((f32[1024,512]{0,1:T(8,128)}), f32[128,512]{0,1:T(8,128)}) %reduce-scatter.49.cloned.1.call-update) | async-done | bytes 262160 | tf_op jit(solution)/shard_map/reduce_scatter | solution.py:172
  663.7 42.9 %reduce-scatter.23.cloned.1.call-done = f32[128,512]{0,1:T(8,128)} async-done(((f32[1024,512]{0,1:T(8,128)}), f32[128,512]{0,1:T(8,128)}) %reduce-scatter.23.cloned.1.call-update) | async-done | bytes 262160 | tf_op jit(solution)/shard_map/reduce_scatter | solution.py:171
  707.6 43.9 %reduce-scatter.25.cloned.1.call-done = f32[128,512]{0,1:T(8,128)} async-done(((f32[1024,512]{0,1:T(8,128)}), f32[128,512]{0,1:T(8,128)}) %reduce-scatter.25.cloned.1.call-update) | async-done | bytes 262160 | tf_op jit(solution)/shard_map/reduce_scatter | solution.py:172
  752.5 43.6 %reduce-scatter.31.cloned.1.call-done = f32[128,512]{0,1:T(8,128)} async-done(((f32[1024,512]{0,1:T(8,128)}), f32[128,512]{0,1:T(8,128)}) %reduce-scatter.31.cloned.1.call-update) | async-done | bytes 262160 | tf_op jit(solution)/shard_map/reduce_scatter | solution.py:171
  797.0 43.8 %reduce-scatter.39.cloned.1.call-done = f32[128,512]{0,1:T(8,128)} async-done(((f32[1024,512]{0,1:T(8,128)}), f32[128,512]{0,1:T(8,128)}) %reduce-scatter.39.cloned.1.call-update) | async-done | bytes 262160 | tf_op jit(solution)/shard_map/reduce_scatter | solution.py:171
  841.8 43.5 %reduce-scatter.41.cloned.1.call-done = f32[128,512]{0,1:T(8,128)} async-done(((f32[1024,512]{0,1:T(8,128)}), f32[128,512]{0,1:T(8,128)}) %reduce-scatter.41.cloned.1.call-update) | async-done | bytes 262160 | tf_op jit(solution)/shard_map/reduce_scatter | solution.py:172
  891.4 38.7 %reduce-scatter.33.cloned.1.call-done = f32[128,512]{0,1:T(8,128)} async-done(((f32[1024,512]{0,1:T(8,128)}), f32[128,512]{0,1:T(8,128)}) %reduce-scatter.33.cloned.1.call-update) | async-done | bytes 262160 | tf_op jit(solution)/shard_map/reduce_scatter | solution.py:172
  1120.6 16.7 reduce-scatter.29.cloned.1.call-done
  1138.9 42.9 %reduce-scatter.35.cloned.1.call-done = f32[128,512]{0,1:T(8,128)} async-done(((f32[1024,512]{0,1:T(8,128)}), f32[128,512]{0,1:T(8,128)}) %reduce-scatter.35.cloned.1.call-update) | async-done | bytes 262160 | tf_op jit(solution)/shard_map/reduce_scatter | solution.py:171
  1183.4 43.3 %reduce-scatter.37.cloned.1.call-done = f32[128,512]{0,1:T(8,128)} async-done(((f32[1024,512]{0,1:T(8,128)}), f32[128,512]{0,1:T(8,128)}) %reduce-scatter.37.cloned.1.call-update) | async-done | bytes 262160 | tf_op jit(solution)/shard_map/reduce_scatter | solution.py:172
  1228.3 42.7 %reduce-scatter.51.cloned.1.call-done = f32[128,512]{0,1:T(8,128)} async-done(((f32[1024,512]{0,1:T(8,128)}), f32[128,512]{0,1:T(8,128)}) %reduce-scatter.51.cloned.1.call-update) | async-done | bytes 262160 | tf_op jit(solution)/shard_map/reduce_scatter | solution.py:171
  1272.7 43.3 %reduce-scatter.53.cloned.1.call-done = f32[128,512]{0,1:T(8,128)} async-done(((f32[1024,512]{0,1:T(8,128)}), f32[128,512]{0,1:T(8,128)}) %reduce-scatter.53.cloned.1.call-update) | async-done | bytes 262160 | tf_op jit(solution)/shard_map/reduce_scatter | solution.py:172
  1333.1 16.3 fusion.3
  1384.1 7.1 maximum_bitcast_fusion.3
  1431.9 20.6 %fusion.1 = f32[3584,2,512]{2,0,1:T(8,128)} fusion(f32[3584,1,512]{2,0,1:T(8,128)} %maximum_bitcast_fusion.1, f32[3584,1,512]{2,0,1:T(8,128)} %maximum_bitcast_fusion, f32[3584,1,512]{2,0,1:T(8,128)} %maximum_bitcast_fusion.3, f32[3584,1,512]{2,0,1:T(8,128)} %maximum_bitcast_fusion.2, f32[3584,1,512]{2,0,1:T(8,128)S(1)} %maximum_bitcast_fusion.5, ...), kind=kLoop, calls=%fused_computation.2 | loop fusion | flops 25690112 | bytes 73400320 | tf_op jit(solution)/shard_map/add | solution.py:343
  1464.7 121.3 %reduce-scatter.61.cloned.1.call-done = f32[16,448]{1,0:T(8,128)} async-done(((f32[512,448]{1,0:T(8,128)}), f32[16,448]{1,0:T(8,128)}) %reduce-scatter.61.cloned.1.call-update) | async-done | bytes 28688
  1587.5 149.6 %reduce-scatter.57.cloned.1.call-done = f32[80,2,512]{2,0,1:T(8,128)} async-done(((f32[2560,2,512]{2,0,1:T(8,128)}), f32[80,2,512]{2,0,1:T(8,128)}) %reduce-scatter.57.cloned.1.call-update) | async-done | bytes 327696 | tf_op jit(solution)/shard_map/reduce_scatter | solution.py:336
  1738.8 158.4 %reduce-scatter.55.cloned.1.call-done = f32[112,2,512]{2,0,1:T(8,128)} async-done(((f32[3584,2,512]{2,0,1:T(8,128)}), f32[112,2,512]{2,0,1:T(8,128)}) %reduce-scatter.55.cloned.1.call-update) | async-done | bytes 458768 | tf_op jit(solution)/shard_map/reduce_scatter | solution.py:335
  1901.5 41.6 %all-reduce = (f32[]{:T(128)}, f32[10,512]{1,0:T(8,128)S(1)}, f32[]{:T(128)}) all-reduce(f32[]{:T(128)S(6)} %add.1031, f32[10,512]{1,0:T(8,128)S(1)} %add_add_fusion.28, f32[]{:T(128)S(6)} %add.1071), channel_id=1, replica_groups=mesh['img'=4,'band'=8] {'img','band'}, use_global_device_ids=true, to_apply=%region_142.143 | all-reduce | flops 5122 | bytes 40976 | tf_op jit(solution)/shard_map/psum | solution.py:347
  (1710 shorter events, 655.5 us)
Async XLA Ops:
  9.2 178.5 %all-gather.43.cloned.1.call-start = ((), (), s32[]{:S(2)}) async-start(), calls=%async_computation.40 | async-start | bytes 1179648 | tf_op jit(solution)/shard_map/all_gather | solution.py:111
  107.2 159.2 %all-gather.37.cloned.1.call-start = ((), (), s32[]{:S(2)}) async-start(), calls=%async_computation.33 | async-start | bytes 1179648 | tf_op jit(solution)/shard_map/all_gather | solution.py:112
  107.8 184.6 %all-gather.27.cloned.1.call-start = ((), (), s32[]{:S(2)}) async-start(), calls=%async_computation.24 | async-start | bytes 1179648 | tf_op jit(solution)/shard_map/all_gather | solution.py:111
  112.3 206.0 %all-gather.29.cloned.1.call-start = ((), (), s32[]{:S(2)}) async-start(), calls=%async_computation.25 | async-start | bytes 1179648 | tf_op jit(solution)/shard_map/all_gather | solution.py:112
  113.1 231.3 %all-gather.51.cloned.1.call-start = ((), (), s32[]{:S(2)}) async-start(), calls=%async_computation.48 | async-start | bytes 1179648 | tf_op jit(solution)/shard_map/all_gather | solution.py:111
  117.6 252.6 %all-gather.53.cloned.1.call-start = ((), (), s32[]{:S(2)}) async-start(), calls=%async_computation.49 | async-start | bytes 1179648 | tf_op jit(solution)/shard_map/all_gather | solution.py:112
  118.2 336.4 %all-gather.21.cloned.1.call-start = ((), (), s32[]{:S(2)}) async-start(), calls=%async_computation.21 | async-start | bytes 1179648 | tf_op jit(solution)/shard_map/all_gather | solution.py:111
  121.7 335.3 %all-gather.31.cloned.1.call-start = ((), (), s32[]{:S(2)}) async-start(), calls=%async_computation.30 | async-start | bytes 1179648 | tf_op jit(solution)/shard_map/all_gather | solution.py:111
  125.2 334.1 %all-gather.47.cloned.1.call-start = ((), (), s32[]{:S(2)}) async-start(), calls=%async_computation.46 | async-start | bytes 1179648 | tf_op jit(solution)/shard_map/all_gather | solution.py:111
  128.7 354.6 %all-gather.23.cloned.1.call-start = ((), (), s32[]{:S(2)}) async-start(), calls=%async_computation.22 | async-start | bytes 1179648 | tf_op jit(solution)/shard_map/all_gather | solution.py:112
  129.3 367.6 %all-gather.33.cloned.1.call-start = ((), (), s32[]{:S(2)}) async-start(), calls=%async_computation.31 | async-start | bytes 1179648 | tf_op jit(solution)/shard_map/all_gather | solution.py:112
  129.9 392.2 %all-gather.49.cloned.1.call-start = ((), (), s32[]{:S(2)}) async-start(), calls=%async_computation.47 | async-start | bytes 1179648 | tf_op jit(solution)/shard_map/all_gather | solution.py:112
  130.4 417.0 %all-gather.39.cloned.1.call-start = ((), (), s32[]{:S(2)}) async-start(), calls=%async_computation.38 | async-start | bytes 1179648 | tf_op jit(solution)/shard_map/all_gather | solution.py:111
  135.7 437.0 %all-gather.41.cloned.1.call-start = ((), (), s32[]{:S(2)}) async-start(), calls=%async_computation.39 | async-start | bytes 1179648 | tf_op jit(solution)/shard_map/all_gather | solution.py:112
  187.4 443.7 %reduce-scatter.47.cloned.1.call-start = ((), (), s32[]{:S(2)}) async-start(), calls=%async_computation.50 | async-start | bytes 2359296 | tf_op jit(solution)/shard_map/reduce_scatter | solution.py:171
  412.1 250.0 %reduce-scatter.49.cloned.1.call-start = ((), (), s32[]{:S(2)}) async-start(), calls=%async_computation.51 | async-start | bytes 2359296 | tf_op jit(solution)/shard_map/reduce_scatter | solution.py:172
  416.7 289.9 %reduce-scatter.23.cloned.1.call-start = ((), (), s32[]{:S(2)}) async-start(), calls=%async_computation.26 | async-start | bytes 2359296 | tf_op jit(solution)/shard_map/reduce_scatter | solution.py:171
  430.9 320.6 %reduce-scatter.25.cloned.1.call-start = ((), (), s32[]{:S(2)}) async-start(), calls=%async_computation.27 | async-start | bytes 2359296 | tf_op jit(solution)/shard_map/reduce_scatter | solution.py:172
  454.5 341.6 %reduce-scatter.31.cloned.1.call-start = ((), (), s32[]{:S(2)}) async-start(), calls=%async_computation.34 | async-start | bytes 2359296 | tf_op jit(solution)/shard_map/reduce_scatter | solution.py:171
  477.1 363.6 %reduce-scatter.39.cloned.1.call-start = ((), (), s32[]{:S(2)}) async-start(), calls=%async_computation.42 | async-start | bytes 2359296 | tf_op jit(solution)/shard_map/reduce_scatter | solution.py:171
  541.6 343.8 %reduce-scatter.41.cloned.1.call-start = ((), (), s32[]{:S(2)}) async-start(), calls=%async_computation.43 | async-start | bytes 2359296 | tf_op jit(solution)/shard_map/reduce_scatter | solution.py:172
  591.3 338.8 %reduce-scatter.33.cloned.1.call-start = ((), (), s32[]{:S(2)}) async-start(), calls=%async_computation.35 | async-start | bytes 2359296 | tf_op jit(solution)/shard_map/reduce_scatter | solution.py:172
  611.9 501.2 %reduce-scatter.43.cloned.1.call-start = ((), (), s32[]{:S(2)}) async-start(), calls=%async_computation.44 | async-start | bytes 2359296 | tf_op jit(solution)/shard_map/reduce_scatter | solution.py:171
  966.3 153.3 %reduce-scatter.27.cloned.1.call-start = ((), (), s32[]{:S(2)}) async-start(), calls=%async_computation.28 | async-start | bytes 2359296 | tf_op jit(solution)/shard_map/reduce_scatter | solution.py:171
  990.2 191.6 %reduce-scatter.35.cloned.1.call-start = ((), (), s32[]{:S(2)}) async-start(), calls=%async_computation.36 | async-start | bytes 2359296 | tf_op jit(solution)/shard_map/reduce_scatter | solution.py:171
  1005.2 221.5 %reduce-scatter.37.cloned.1.call-start = ((), (), s32[]{:S(2)}) async-start(), calls=%async_computation.37 | async-start | bytes 2359296 | tf_op jit(solution)/shard_map/reduce_scatter | solution.py:172
  1010.2 260.9 %reduce-scatter.51.cloned.1.call-start = ((), (), s32[]{:S(2)}) async-start(), calls=%async_computation.52 | async-start | bytes 2359296 | tf_op jit(solution)/shard_map/reduce_scatter | solution.py:171
  1025.3 290.7 %reduce-scatter.53.cloned.1.call-start = ((), (), s32[]{:S(2)}) async-start(), calls=%async_computation.53 | async-start | bytes 2359296 | tf_op jit(solution)/shard_map/reduce_scatter | solution.py:172
  1039.5 421.1 %reduce-scatter.59.cloned.1.call-start = ((), (), s32[]{:S(2)}) async-start(), calls=%async_computation.56 | async-start | bytes 1081344 | tf_op jit(solution)/shard_map/reduce_scatter | solution.py:338
  1067.6 518.4 %reduce-scatter.61.cloned.1.call-start = ((), (), s32[]{:S(2)}) async-start(), calls=%async_computation.57 | async-start | bytes 1081344
  1328.1 409.0 %reduce-scatter.57.cloned.1.call-start = ((), (), s32[]{:S(2)}) async-start(), calls=%async_computation.55 | async-start | bytes 10813440 | tf_op jit(solution)/shard_map/reduce_scatter | solution.py:336
  1349.5 547.7 %reduce-scatter.55.cloned.1.call-start = ((), (), s32[]{:S(2)}) async-start(), calls=%async_computation.54 | async-start | bytes 15138816 | tf_op jit(solution)/shard_map/reduce_scatter | solution.py:335
  (588 other events, 14866.3 us)
Sparse Core Ops, SparseCore 0:
  11.5 79.7 all-gather.18
  124.4 23.4 all-gather.44
  151.3 65.7 all-gather.24
  242.9 23.4 all-gather.36
  268.9 23.4 all-gather.26
  320.8 23.4 all-gather.50
  346.7 23.4 all-gather.52
  372.1 23.4 all-gather.20
  422.8 23.5 all-gather.46
  448.1 23.4 all-gather.22
  498.6 23.4 all-gather.48
  523.8 23.5 all-gather.38
  576.0 41.2 reduce-scatter.46
  620.7 41.3 reduce-scatter.48
  665.4 41.2 reduce-scatter.22
  710.2 41.2 reduce-scatter.24
  754.8 41.2 reduce-scatter.30
  799.5 41.2 reduce-scatter.38
  844.1 41.2 reduce-scatter.40
  888.8 41.2 reduce-scatter.32
  961.9 41.2 reduce-scatter.42
  1006.8 41.2 reduce-scatter.44
  1051.3 41.2 reduce-scatter.26
  1096.0 41.2 reduce-scatter.28
  1140.6 41.2 reduce-scatter.34
  1185.5 41.2 reduce-scatter.36
  1229.9 41.1 reduce-scatter.50
  1274.7 41.2 reduce-scatter.52
  1318.2 134.7 reduce-scatter.58
  1455.3 130.6 reduce-scatter.60
  1588.2 148.9 reduce-scatter.56
  1739.4 157.7 reduce-scatter.54
  (6 shorter events, 137.0 us)
where the time goes:
time: 1990 us; the launch traced here: 1970 us
  waiting for transfers between devices  1080 us (54%)
  matrix products  372 us (19%)
  other arithmetic  201 us (10%)
  blocking collectives  164 us (8%)
  local copies, waits for them, and re-layouts  117 us (6%)
  between operations  37.7 us (2%)
    reduce_scatter x8, waiting for transfers between devices, block_backward(): lax.psum_scatter(grad_values, 'band', scatter_dimension=0, tiled=True)  259 us
    reduce_scatter x8, waiting for transfers between devices, block_backward(): lax.psum_scatter(grad_keys, 'band', scatter_dimension=0, tiled=True)  216 us
    reduce_scatter x1, waiting for transfers between devices, body(): lax.psum_scatter(local_grads[0], ('img', 'band'), scatter_dimension=0, ti...  158 us
    reduce_scatter x1, waiting for transfers between devices, body(): lax.psum_scatter(local_grads[1], ('img', 'band'), scatter_dimension=0, ti...  150 us
    unnamed x39, waiting for transfers between devices  126 us
    all_gather x8, waiting for transfers between devices, block_forward(): lax.all_gather(projected[:, 2 * model_width:], 'band', axis=0, tiled=True)  116 us
    dot_general x48, matrix products, matmul_plain(): return jnp.dot(first_op, second_op, preferred_element_type=jnp.float32)  83.3 us
    dot_general x48, matrix products, matmul_outer(): lax.dot_general(first_op, second_op, (((0,), (0,)), ((), ())), preferred_...  81.2 us
  transfers between devices with their start and end apart: 38, of which 26 were waited for; matrix products, arithmetic and copies ran while one was open for 30% of the time, Pallas kernels for 0%

commit v1 on v0

--- a/solution.py
+++ b/solution.py
@@ -1,10 +1,15 @@
+import functools
+
 import jax
 import jax.numpy as jnp
 from jax import lax
+from jax.experimental import pallas as pl
+from jax.experimental.pallas import tpu as pltpu
 from jax.sharding import PartitionSpec as P
 
 HEADS = 8
 HDIM = 64
+MESH = pl.DeviceIdType.MESH
 
 
 norm_eps = 1e-05
@@ -99,21 +104,19 @@
         grad_q.reshape(queries.shape[0], -1),
         grad_k.reshape(key_rows.shape[0], -1),
         grad_v.reshape(key_rows.shape[0], -1),
-        row_dot[..., 0],
-    )
-
-
-def block_forward(hidden, wide_rows, narrow_rows, gain_rows, allowed):
-    model_width = hidden.shape[1]
-    normed = layer_norm(hidden, gain_rows[0], gain_rows[1]).astype(jnp.bfloat16)
-    projected = matmul_trans(normed, wide_rows[: 3 * model_width]).astype(jnp.bfloat16)
-    keys_values = (
-        lax.all_gather(projected[:, model_width : 2 * model_width], "band", axis=0, tiled=True),
-        lax.all_gather(projected[:, 2 * model_width :], "band", axis=0, tiled=True),
-    )
-    attended, log_total = attend(
-        projected[:, :model_width], keys_values[0], keys_values[1], allowed
-    )
+    )
+
+
+def block_forward(hidden_all, part, wide_rows, narrow_rows, gain_rows, allowed):
+    model_width = hidden_all.shape[1]
+    own_rows = allowed.shape[0]
+    normed_all = layer_norm(hidden_all, gain_rows[0], gain_rows[1]).astype(jnp.bfloat16)
+    hidden = lax.dynamic_slice_in_dim(hidden_all, part * own_rows, own_rows, 0)
+    normed = lax.dynamic_slice_in_dim(normed_all, part * own_rows, own_rows, 0)
+    queries = matmul_trans(normed, wide_rows[:model_width]).astype(jnp.bfloat16)
+    key_rows = matmul_trans(normed_all, wide_rows[model_width : 2 * model_width]).astype(jnp.bfloat16)
+    value_rows = matmul_trans(normed_all, wide_rows[2 * model_width : 3 * model_width]).astype(jnp.bfloat16)
+    attended, log_total = attend(queries, key_rows, value_rows, allowed)
     middle = hidden + matmul_plain(attended, narrow_rows[:model_width])
     second = layer_norm(middle, gain_rows[2], gain_rows[3]).astype(jnp.bfloat16)
     upper_in = matmul_trans(second, wide_rows[3 * model_width :])
@@ -121,34 +124,12 @@
     result = middle + matmul_plain(active, narrow_rows[model_width:])
     return (
         result,
-        (
-            hidden,
-            normed,
-            projected,
-            keys_values,
-            attended,
-            log_total,
-            middle,
-            second,
-            upper_in,
-            active,
-        ),
-    )
-
-
-def block_backward(grad_out, wide_rows, narrow_rows, gain_rows, allowed, saved):
-    (
-        hidden,
-        normed,
-        projected,
-        keys_values,
-        attended,
-        log_total,
-        middle,
-        second,
-        upper_in,
-        active,
-    ) = saved
+        (hidden, normed, queries, key_rows, value_rows, attended, log_total, middle, second, upper_in, active),
+    )
+
+
+def block_backward(grad_out, wide_rows, narrow_rows, gain_rows, allowed, saved, groups):
+    (hidden, normed, queries, key_rows, value_rows, attended, log_total, middle, second, upper_in, active) = saved
     model_width = hidden.shape[1]
     grad_y = grad_out.astype(jnp.bfloat16)
     grad_down = matmul_outer(active, grad_y)
@@ -163,14 +144,11 @@
     grad_attn = grad_mid.astype(jnp.bfloat16)
     grad_outproj = matmul_outer(attended, grad_attn)
     grad_att = matmul_trans(grad_attn, narrow_rows[:model_width]).astype(jnp.bfloat16)
-    queries = projected[:, :model_width]
-    grad_q, grad_keys, grad_values, row_dot = attend_back(
-        queries, keys_values[0], keys_values[1], allowed, log_total, grad_att
-    )
-    grad_k, grad_v = (
-        lax.psum_scatter(grad_keys, "band", scatter_dimension=0, tiled=True),
-        lax.psum_scatter(grad_values, "band", scatter_dimension=0, tiled=True),
-    )
+    grad_q, grad_keys, grad_values = attend_back(
+        queries, key_rows, value_rows, allowed, log_total, grad_att
+    )
+    grad_k = lax.psum_scatter(grad_keys, "band", scatter_dimension=0, tiled=True, axis_index_groups=groups)
+    grad_v = lax.psum_scatter(grad_values, "band", scatter_dimension=0, tiled=True, axis_index_groups=groups)
     grad_mixed = jnp.concatenate([grad_q, grad_k, grad_v], axis=1).astype(jnp.bfloat16)
     grad_qkv = matmul_outer(grad_mixed, normed)
     _, first_back = jax.vjp(layer_norm, hidden, gain_rows[0], gain_rows[1])
@@ -186,70 +164,403 @@
     )
 
 
-def micro_step(gathered, norms, pixel_rows, valid_rows, code_rows, allowed, count, latent_total):
-    wide_all, narrow_all, edge_all, book_all = gathered
-    patch_size = pixel_rows.shape[1]
-    code_width = book_all.shape[1]
+def pick_codes(code_rows, book_wide, code_width):
+    fold = book_wide.shape[1] // code_width
+    one_hot = (
+        (code_rows // fold)[:, None] == jnp.arange(book_wide.shape[0], dtype=jnp.int32)[None, :]
+    ).astype(jnp.bfloat16)
+    lane_fold = jnp.arange(book_wide.shape[1], dtype=jnp.int32)[None, :] // code_width
+    lane_mask = (code_rows % fold)[:, None] == lane_fold
+    spread = jnp.where(lane_mask, matmul_plain(one_hot, book_wide), 0.0)
+    chosen = sum(spread[:, k * code_width : (k + 1) * code_width] for k in range(fold))
+    return chosen, one_hot, lane_mask
+
+
+def row_step(gathered, norms, pixel_all, valid_rows, code_all, part, allowed, count, latent_total, groups):
+    wide_all, narrow_all, edge_all, book_wide = gathered
+    patch_size = pixel_all.shape[1]
+    code_width = edge_all.shape[1] // 2 - patch_size
+    own_rows = allowed.shape[0]
     edge_in = edge_all[:, :patch_size]
     edge_pix = edge_all[:, patch_size : 2 * patch_size]
     edge_qin = edge_all[:, 2 * patch_size : 2 * patch_size + code_width]
     edge_qout = edge_all[:, 2 * patch_size + code_width :]
-    start = matmul_trans(pixel_rows, edge_in)
-    encoded, enc_saved = block_forward(start, wide_all[:, 0], narrow_all[:, 0], norms[0:4], allowed)
-    encoded_low = encoded.astype(jnp.bfloat16)
-    latent = matmul_plain(encoded_low, edge_qin)
-    one_hot = (
-        code_rows[:, None] == jnp.arange(book_all.shape[0], dtype=jnp.int32)[None, :]
-    ).astype(jnp.bfloat16)
-    chosen = matmul_plain(one_hot, book_all)
+    pixel_rows = lax.dynamic_slice_in_dim(pixel_all, part * own_rows, own_rows, 0)
+    chosen_all, one_hot_all, lane_mask_all = pick_codes(code_all, book_wide, code_width)
+    chosen_low_all = chosen_all.astype(jnp.bfloat16)
+    chosen = lax.dynamic_slice_in_dim(chosen_all, part * own_rows, own_rows, 0)
+    one_hot = lax.dynamic_slice_in_dim(one_hot_all, part * own_rows, own_rows, 0)
+    lane_mask = lax.dynamic_slice_in_dim(lane_mask_all, part * own_rows, own_rows, 0)
     chosen_low = chosen.astype(jnp.bfloat16)
-    begin = matmul_trans(chosen_low, edge_qout)
-    decoded, dec_saved = block_forward(begin, wide_all[:, 1], narrow_all[:, 1], norms[4:8], allowed)
+    begin = matmul_trans(chosen_low_all, edge_qout)
+    decoded, dec_saved = block_forward(begin, part, wide_all[1], narrow_all[1], norms[4:8], allowed)
     final = layer_norm(decoded, norms[8], norms[9]).astype(jnp.bfloat16)
     predict = matmul_plain(final, edge_pix)
     error = predict - pixel_rows.astype(jnp.float32)
     pixel_mask = valid_rows.astype(jnp.float32)
-    gap = chosen - latent
-    loss_part = (
-        jnp.sum(pixel_mask * (error * error + jnp.abs(error))) / count
-        + (1.0 + commitment) * jnp.sum(gap * gap) / latent_total
-    )
+    loss_pix = jnp.sum(pixel_mask * (error * error + jnp.abs(error))) / count
     grad_pred = (pixel_mask * (2.0 * error + jnp.sign(error)) / count).astype(jnp.bfloat16)
     grad_pixw = matmul_outer(final, grad_pred)
     _, final_back = jax.vjp(layer_norm, decoded, norms[8], norms[9])
     grad_dec, gain_last, offset_last = final_back(matmul_trans(grad_pred, edge_pix))
     grad_begin, dec_wide, dec_narrow, dec_gains = block_backward(
-        grad_dec, wide_all[:, 1], narrow_all[:, 1], norms[4:8], allowed, dec_saved
+        grad_dec, wide_all[1], narrow_all[1], norms[4:8], allowed, dec_saved, groups
     )
     grad_begin_low = grad_begin.astype(jnp.bfloat16)
     grad_qout = matmul_outer(grad_begin_low, chosen_low)
+    start = matmul_trans(pixel_all, edge_in)
+    encoded, enc_saved = block_forward(start, part, wide_all[0], narrow_all[0], norms[0:4], allowed)
+    encoded_low = encoded.astype(jnp.bfloat16)
+    latent = matmul_plain(encoded_low, edge_qin)
+    gap = chosen - latent
+    loss_part = loss_pix + (1.0 + commitment) * jnp.sum(gap * gap) / latent_total
     grad_latent = (
         matmul_plain(grad_begin_low, edge_qout) - 2.0 * commitment * gap / latent_total
     ).astype(jnp.bfloat16)
-    grad_book = lax.dot_general(
-        one_hot.astype(jnp.float32),
-        2.0 * gap / latent_total,
-        (((0,), (0,)), ((), ())),
-        precision=highest,
-    )
+    fold = lane_mask.shape[1] // code_width
+    gap_wide = jnp.where(lane_mask, jnp.tile(2.0 * gap / latent_total, (1, fold)), 0.0)
+    gap_high = gap_wide.astype(jnp.bfloat16)
+    gap_rest = gap_wide - gap_high.astype(jnp.float32)
+    gap_middle = gap_rest.astype(jnp.bfloat16)
+    gap_low = (gap_rest - gap_middle.astype(jnp.float32)).astype(jnp.bfloat16)
+    grad_book = (
+        matmul_outer(one_hot, gap_high) + matmul_outer(one_hot, gap_middle)
+    ) + matmul_outer(one_hot, gap_low)
     grad_qin = matmul_outer(encoded_low, grad_latent)
     grad_start, enc_wide, enc_narrow, enc_gains = block_backward(
-        matmul_trans(grad_latent, edge_qin),
-        wide_all[:, 0],
-        narrow_all[:, 0],
-        norms[0:4],
-        allowed,
-        enc_saved,
+        matmul_trans(grad_latent, edge_qin), wide_all[0], narrow_all[0], norms[0:4], allowed, enc_saved, groups
     )
     grad_inw = matmul_outer(grad_start.astype(jnp.bfloat16), pixel_rows)
     grads = (
-        jnp.stack([enc_wide, dec_wide], axis=1),
-        jnp.stack([enc_narrow, dec_narrow], axis=1),
+        enc_wide, dec_wide, enc_narrow, dec_narrow,
         jnp.concatenate([grad_inw, grad_pixw, grad_qin, grad_qout], axis=1),
         grad_book,
     )
     norm_grad = jnp.concatenate([enc_gains, dec_gains, gain_last[None], offset_last[None]], axis=0)
     return (grads, norm_grad, loss_part)
+
+
+def place():
+    img_at = lax.axis_index("img")
+    band_at = lax.axis_index("band")
+    return img_at, band_at, band_at // 4, (band_at // 2) % 2, band_at % 2
+
+
+def peers(img_at, band_at):
+    found = [((img_at + step) % 4, band_at) for step in range(1, 4)]
+    return found + [(img_at, (band_at + step) % 8) for step in range(1, 8)]
+
+
+def meet(img_at, band_at):
+    barrier = pltpu.get_barrier_semaphore()
+    for peer in peers(img_at, band_at):
+        pl.semaphore_signal(barrier, inc=1, device_id=peer, device_id_type=MESH)
+    pl.semaphore_wait(barrier, 10)
+
+
+def far_copy(src, dst, send, recv, target):
+    return pltpu.make_async_remote_copy(
+        src_ref=src, dst_ref=dst, send_sem=send, recv_sem=recv, device_id=target, device_id_type=MESH
+    )
+
+
+def sum_everywhere(own_ref, img_buf, band_buf, send, recv, img_at, band_at, result_ref):
+    img_buf[img_at] = own_ref[...]
+    first = [
+        far_copy(own_ref, img_buf.at[img_at], send.at[step], recv.at[step], ((img_at + step) % 4, band_at))
+        for step in range(1, 4)
+    ]
+    for copy in first:
+        copy.start()
+    for copy in first:
+        copy.wait()
+    result_ref[...] = (img_buf[0] + img_buf[1]) + (img_buf[2] + img_buf[3])
+    band_buf[band_at] = result_ref[...]
+    second = [
+        far_copy(
+            result_ref, band_buf.at[band_at], send.at[3 + step], recv.at[3 + step], (img_at, (band_at + step) % 8)
+        )
+        for step in range(1, 8)
+    ]
+    for copy in second:
+        copy.start()
+    for copy in second:
+        copy.wait()
+    total = band_buf[0]
+    for k in range(1, 8):
+        total = total + band_buf[k]
+    result_ref[...] = total
+
+
+def gather_kernel(cuts, *refs):
+    count = len(cuts)
+    shards, (slab, code, tally) = refs[:count], refs[count : count + 3]
+    wholes = refs[count + 3 : 2 * count + 3]
+    slab_all, code_all, tally_all = refs[2 * count + 3 : 2 * count + 6]
+    (img_buf, band_buf, near, z_send, z_recv, p_send, p_recv, e_send, e_recv, t_send, t_recv) = refs[2 * count + 6 :]
+    img_at, band_at, y_at, x_at, c_at = place()
+    chip_at = band_at // 2
+    over_y = (img_at, band_at + 4 - 8 * y_at)
+    over_x = (img_at, band_at + 2 - 4 * x_at)
+    over_c = (img_at, band_at + 1 - 2 * c_at)
+    meet(img_at, band_at)
+    exchange = []
+    for step in range(1, 4):
+        chip = (chip_at + step) % 4
+        for k, (src, dst) in enumerate(((slab, slab_all), (code, code_all))):
+            exchange.append(
+                far_copy(
+                    src.at[chip], dst.at[chip_at, c_at], e_send.at[k, step], e_recv.at[k, step],
+                    (img_at, 2 * chip + c_at),
+                )
+            )
+    for k, (src, dst) in enumerate(((slab, slab_all), (code, code_all))):
+        exchange.append(pltpu.make_async_copy(src.at[chip_at], dst.at[chip_at, c_at], near.at[count + k]))
+    for copy in exchange:
+        copy.start()
+
+    def along_z(p):
+        here = wholes[p].at[img_at, y_at, x_at, c_at]
+        copies = [
+            far_copy(shards[p], here, z_send.at[p, step], z_recv.at[p, step], ((img_at + step) % 4, band_at))
+            for step in range(1, 4)
+        ]
+        return copies + [pltpu.make_async_copy(shards[p], here, near.at[p])]
+
+    def along_first(p):
+        cut, rows = cuts[p], shards[p].shape[0]
+        copies = []
+        if cut > 0:
+            part = wholes[p].at[:, y_at, x_at, c_at, pl.ds(0, cut)]
+            copies.append(far_copy(part, part, p_send.at[p, 0], p_recv.at[p, 0], over_y))
+        if cut < rows:
+            part = wholes[p].at[:, y_at, x_at, c_at, pl.ds(cut, rows - cut)]
+            copies.append(far_copy(part, part, p_send.at[p, 1], p_recv.at[p, 1], over_x))
+        return copies
+
+    def along_second(p):
+        cut, rows = cuts[p], shards[p].shape[0]
+        copies = []
+        if cut > 0:
+            part = wholes[p].at[:, :, x_at, c_at, pl.ds(0, cut)]
+            copies.append(far_copy(part, part, p_send.at[p, 2], p_recv.at[p, 2], over_x))
+        if cut < rows:
+            part = wholes[p].at[:, y_at, :, c_at, pl.ds(cut, rows - cut)]
+            copies.append(far_copy(part, part, p_send.at[p, 3], p_recv.at[p, 3], over_y))
+        return copies
+
+    def along_core(p):
+        part = wholes[p].at[:, :, :, c_at]
+        return [far_copy(part, part, p_send.at[p, 4], p_recv.at[p, 4], over_c)]
+
+    stages = (along_z, along_first, along_second, along_core)
+    flying = {}
+
+    def launch(p, k):
+        flying[p, k] = stages[k](p)
+        for copy in flying[p, k]:
+            copy.start()
+
+    def land(p, k):
+        for copy in flying.pop((p, k)):
+            copy.wait()
+
+    for p in range(count):
+        launch(p, 0)
+    for copy in exchange:
+        copy.wait()
+    late = []
+    for k, dst in enumerate((slab_all, code_all)):
+        part = dst.at[:, c_at]
+        late.append(far_copy(part, part, e_send.at[k, 0], e_recv.at[k, 0], over_c))
+    for copy in late:
+        copy.start()
+    sum_everywhere(tally, img_buf, band_buf, t_send, t_recv, img_at, band_at, tally_all)
+    for beat in range(count + 3):
+        for k in range(4):
+            p = beat - k
+            if 0 <= p < count:
+                land(p, k)
+                if k < 3:
+                    launch(p, k + 1)
+    for copy in late:
+        copy.wait()
+
+
+def gather_all(shards, cuts, slab, code, tally):
+    any_space = pl.BlockSpec(memory_space=pl.ANY)
+    vmem_space = pl.BlockSpec(memory_space=pltpu.VMEM)
+    count = len(shards)
+    out_shape = [jax.ShapeDtypeStruct((4, 2, 2, 2) + s.shape, s.dtype) for s in shards]
+    out_shape += [
+        jax.ShapeDtypeStruct((4, 2) + slab.shape[1:], slab.dtype),
+        jax.ShapeDtypeStruct((4, 2) + code.shape[1:], code.dtype),
+        jax.ShapeDtypeStruct(tally.shape, tally.dtype),
+    ]
+    dma = pltpu.SemaphoreType.DMA
+    return pl.pallas_call(
+        functools.partial(gather_kernel, cuts),
+        out_shape=out_shape,
+        in_specs=[any_space] * (count + 2) + [vmem_space],
+        out_specs=[any_space] * (count + 2) + [vmem_space],
+        scratch_shapes=[
+            pltpu.VMEM((4,) + tally.shape, tally.dtype),
+            pltpu.VMEM((8,) + tally.shape, tally.dtype),
+            dma((count + 2,)),
+            dma((count, 4)), dma((count, 4)),
+            dma((count, 5)), dma((count, 5)),
+            dma((2, 4)), dma((2, 4)),
+            dma((11,)), dma((11,)),
+        ],
+        compiler_params=pltpu.CompilerParams(collective_id=0, has_side_effects=True),
+        name="gather_all",
+    )(*shards, slab, code, tally)
+
+
+def reduce_kernel(cuts, *refs):
+    count = len(cuts)
+    grads, small = refs[:count], refs[count]
+    shares = refs[count + 1 : 2 * count + 1]
+    small_all = refs[2 * count + 1]
+    rest = refs[2 * count + 2 :]
+    own, pair = rest[:count], rest[count : 2 * count]
+    first_a, first_b = rest[2 * count : 3 * count], rest[3 * count : 4 * count]
+    second_a, second_b = rest[4 * count : 5 * count], rest[5 * count : 6 * count]
+    last = rest[6 * count : 7 * count]
+    (img_buf, band_buf, small_own, near, p_send, p_recv, z_send, z_recv, t_send, t_recv) = rest[7 * count :]
+    img_at, band_at, y_at, x_at, c_at = place()
+    over_y = (img_at, band_at + 4 - 8 * y_at)
+    over_x = (img_at, band_at + 2 - 4 * x_at)
+    over_c = (img_at, band_at + 1 - 2 * c_at)
+    meet(img_at, band_at)
+
+    def along_core(p):
+        return [
+            far_copy(grads[p].at[:, :, :, 1 - c_at], pair[p], p_send.at[p, 0], p_recv.at[p, 0], over_c),
+            pltpu.make_async_copy(grads[p].at[:, :, :, c_at], own[p], near.at[p]),
+        ]
+
+    def add_core(p):
+        def step(k, carry):
+            z, yx = k // 4, k % 4
+            own[p][z, yx // 2, yx % 2] += pair[p][z, yx // 2, yx % 2]
+            return carry
+        lax.fori_loop(0, 16, step, 0)
+
+    def spans(p):
+        rows = own[p].shape[3]
+        return pl.ds(0, cuts[p]), pl.ds(cuts[p], rows - cuts[p])
+
+    def along_first(p):
+        rows_a, rows_b = spans(p)
+        return [
+            far_copy(own[p].at[:, :, 1 - x_at, rows_a], first_a[p], p_send.at[p, 1], p_recv.at[p, 1], over_x),
+            far_copy(own[p].at[:, 1 - y_at, :, rows_b], first_b[p], p_send.at[p, 2], p_recv.at[p, 2], over_y),
+        ]
+
+    def add_first(p):
+        rows_a, rows_b = spans(p)
+        def step(k, carry):
+            z, w = k // 2, k % 2
+            own[p][z, w, x_at, rows_a] += first_a[p][z, w]
+            own[p][z, y_at, w, rows_b] += first_b[p][z, w]
+            return carry
+        lax.fori_loop(0, 8, step, 0)
+
+    def along_second(p):
+        rows_a, rows_b = spans(p)
+        return [
+            far_copy(own[p].at[:, 1 - y_at, x_at, rows_a], second_a[p], p_send.at[p, 3], p_recv.at[p, 3], over_y),
+            far_copy(own[p].at[:, y_at, 1 - x_at, rows_b], second_b[p], p_send.at[p, 4], p_recv.at[p, 4], over_x),
+        ]
+
+    def add_second(p):
+        rows_a, rows_b = spans(p)
+        def step(z, carry):
+            own[p][z, y_at, x_at, rows_a] += second_a[p][z]
+            own[p][z, y_at, x_at, rows_b] += second_b[p][z]
+            return carry
+        lax.fori_loop(0, 4, step, 0)
+
+    def along_z(p):
+        copies = []
+        for step in range(1, 4):
+            target = (img_at + step) % 4
+            copies.append(
+                far_copy(
+                    own[p].at[target, y_at, x_at], last[p].at[step - 1],
+                    z_send.at[p, step], z_recv.at[p, step], (target, band_at),
+                )
+            )
+        return copies
+
+    def add_z(p):
+        shares[p][...] = (own[p][img_at, y_at, x_at] + last[p][0]) + (last[p][1] + last[p][2])
+
+    stages = (along_core, along_first, along_second, along_z)
+    adds = (add_core, add_first, add_second, add_z)
+    flying = {}
+
+    def launch(p, k):
+        flying[p, k] = stages[k](p)
+        for copy in flying[p, k]:
+            copy.start()
+
+    def land(p, k):
+        for copy in flying.pop((p, k)):
+            copy.wait()
+        adds[k](p)
+
+    for p in range(count):
+        launch(p, 0)
+    for beat in range(count + 3):
+        for k in range(4):
+            p = beat - k
+            if 0 <= p < count:
+                land(p, k)
+                if k < 3:
+                    launch(p, k + 1)
+    squares = sum(jnp.sum(share[...] * share[...]) for share in shares)
+    shape = small.shape
+    at_spot = (lax.broadcasted_iota(jnp.int32, shape, 0) == 11) & (lax.broadcasted_iota(jnp.int32, shape, 1) == 0)
+    small_own[...] = small[...] + jnp.where(at_spot, squares, 0.0)
+    sum_everywhere(small_own, img_buf, band_buf, t_send, t_recv, img_at, band_at, small_all)
+
+
+def reduce_all(grads, cuts, small):
+    any_space = pl.BlockSpec(memory_space=pl.ANY)
+    vmem_space = pl.BlockSpec(memory_space=pltpu.VMEM)
+    count = len(grads)
+    rows = [g.shape[4] for g in grads]
+    wide = [g.shape[5] for g in grads]
+    f32 = jnp.float32
+    dma = pltpu.SemaphoreType.DMA
+    scratch = [pltpu.VMEM((4, 2, 2, r, w), f32) for r, w in zip(rows, wide)]
+    scratch += [pltpu.VMEM((4, 2, 2, r, w), f32) for r, w in zip(rows, wide)]
+    scratch += [pltpu.VMEM((4, 2, a, w), f32) for a, w in zip(cuts, wide)]
+    scratch += [pltpu.VMEM((4, 2, r - a, w), f32) for a, r, w in zip(cuts, rows, wide)]
+    scratch += [pltpu.VMEM((4, a, w), f32) for a, w in zip(cuts, wide)]
+    scratch += [pltpu.VMEM((4, r - a, w), f32) for a, r, w in zip(cuts, rows, wide)]
+    scratch += [pltpu.VMEM((3, r, w), f32) for r, w in zip(rows, wide)]
+    scratch += [
+        pltpu.VMEM((4,) + small.shape, f32),
+        pltpu.VMEM((8,) + small.shape, f32),
+        pltpu.VMEM(small.shape, f32),
+        dma((count,)),
+        dma((count, 5)), dma((count, 5)),
+        dma((count, 4)), dma((count, 4)),
+        dma((11,)), dma((11,)),
+    ]
+    return pl.pallas_call(
+        functools.partial(reduce_kernel, cuts),
+        out_shape=[jax.ShapeDtypeStruct((r, w), f32) for r, w in zip(rows, wide)]
+        + [jax.ShapeDtypeStruct(small.shape, f32)],
+        in_specs=[any_space] * count + [vmem_space],
+        out_specs=[vmem_space] * (count + 1),
+        scratch_shapes=scratch,
+        compiler_params=pltpu.CompilerParams(collective_id=1, has_side_effects=True, vmem_limit_bytes=56 << 20),
+        name="reduce_all",
+    )(*grads, small)
 
 
 def moments(gradient, first_old, second_old):
@@ -298,53 +609,78 @@
     row_count = pixels.shape[2]
     length = row_count * band_count
     batch_count = pixels.shape[0]
+    group = band_count // batch_count
+    row = band_index // group
+    part = band_index % group
+    own_rows = length // group
+    groups = [[k * group + j for j in range(group)] for k in range(batch_count)]
     layer_count = w_wide.shape[1]
-    latent_total = batch_count * lax.axis_size("img") * length * codebook.shape[1]
-    shards = (
-        w_wide.astype(jnp.bfloat16),
-        w_narrow.astype(jnp.bfloat16),
-        w_edge.astype(jnp.bfloat16),
-        codebook.astype(jnp.bfloat16),
-    )
-    count = lax.psum(jnp.sum(valid.astype(jnp.float32)), ("img", "band"))
+    code_width = codebook.shape[1]
+    latent_total = batch_count * lax.axis_size("img") * length * code_width
+    both = ("img", "band")
+
+    direct = band_count == 8 and lax.axis_size("img") == 4 and batch_count == 4
+    shards = [w_wide[:, l].astype(jnp.bfloat16) for l in range(layer_count)]
+    shards += [w_narrow[:, l].astype(jnp.bfloat16) for l in range(layer_count)]
+    shards += [w_edge.astype(jnp.bfloat16), codebook.astype(jnp.bfloat16).reshape(-1, 4 * code_width)]
+    slab = jnp.concatenate([pixels[:, 0], valid[:, 0].astype(jnp.bfloat16)], axis=2)
+    local_count = jnp.sum(valid.astype(jnp.float32))
+    patch_size = pixels.shape[3]
+    if direct:
+        order = (5, 4, 1, 3, 0, 2)
+        cuts = tuple({112: 64, 80: 32, 16: 16, 64: 0}[shards[k].shape[0]] for k in order)
+        moved = gather_all([shards[k] for k in order], cuts, slab, codes, jnp.full((8, 128), local_count))
+        wholes = [None] * 6
+        for k, value in zip(order, moved):
+            wholes[k] = value.reshape((-1, value.shape[-1]))
+        slab_all = moved[6].reshape(length, -1)
+        code_all = moved[7].reshape(length)
+        count = moved[8][0, 0]
+    else:
+        wholes = [lax.all_gather(shard, both, axis=0, tiled=True) for shard in shards]
+        count = lax.psum(local_count, both)
+
+        def whole_row(local):
+            everywhere = lax.all_gather(local, "band", axis=0)
+            chosen_row = lax.dynamic_index_in_dim(everywhere, row, axis=1, keepdims=False)
+            return chosen_row.reshape((length,) + local.shape[2:])
+
+        slab_all = whole_row(slab)
+        code_all = whole_row(codes[:, 0])
+    gathered = (wholes[:2], wholes[2:4], wholes[4], wholes[5])
+    pixel_all = slab_all[:, :patch_size]
+    valid_rows = lax.dynamic_slice_in_dim(slab_all, part * own_rows, own_rows, 0)[:, patch_size:]
     positions = jnp.arange(length, dtype=jnp.int32)
-    own_positions = band_index * row_count + jnp.arange(row_count, dtype=jnp.int32)
-    grad_sum = None
-    norm_sum = None
-    loss_sum = None
-    for batch_index in range(batch_count):
-        gathered = (
-            lax.all_gather(shards[0], ("img", "band"), axis=0, tiled=True),
-            lax.all_gather(shards[1], ("img", "band"), axis=0, tiled=True),
-            lax.all_gather(shards[2], ("img", "band"), axis=0, tiled=True),
-            lax.all_gather(shards[3], ("img", "band"), axis=0, tiled=True),
-        )
-        span = jnp.where(image_kind[batch_index, 0] == 0, length, length // 4)
-        allowed = (own_positions // span)[:, None] == (positions // span)[None, :]
-        local_grads, norm_grad, loss_part = micro_step(
-            gathered,
-            norms,
-            pixels[batch_index, 0],
-            valid[batch_index, 0],
-            codes[batch_index, 0],
-            allowed,
-            count,
-            latent_total,
-        )
-        local_grads = (
-            lax.psum_scatter(local_grads[0], ("img", "band"), scatter_dimension=0, tiled=True),
-            lax.psum_scatter(local_grads[1], ("img", "band"), scatter_dimension=0, tiled=True),
-            lax.psum_scatter(local_grads[2], ("img", "band"), scatter_dimension=0, tiled=True),
-            lax.psum_scatter(local_grads[3], ("img", "band"), scatter_dimension=0, tiled=True),
-        )
-        if grad_sum is None:
-            grad_sum, norm_sum, loss_sum = (local_grads, norm_grad, loss_part)
-        else:
-            grad_sum = jax.tree.map(jnp.add, grad_sum, local_grads)
-            norm_sum = norm_sum + norm_grad
-            loss_sum = loss_sum + loss_part
-    squares = sum((jnp.sum(member * member) for member in grad_sum))
-    norm_total, square_total, loss_total = lax.psum((norm_sum, squares, loss_sum), ("img", "band"))
+    own_positions = part * own_rows + jnp.arange(own_rows, dtype=jnp.int32)
+    kind = lax.dynamic_index_in_dim(image_kind[:, 0], row, 0, keepdims=False)
+    span = jnp.where(kind == 0, length, length // 4)
+    allowed = (own_positions // span)[:, None] == (positions // span)[None, :]
+    local_grads, norm_sum, loss_sum = row_step(
+        gathered, norms, pixel_all, valid_rows, code_all, part, allowed, count, latent_total, groups
+    )
+    if direct:
+        blocks = [g.reshape((4, 2, 2, 2, g.shape[0] // 32, g.shape[1])) for g in local_grads]
+        order = (1, 3, 0, 2, 4, 5)
+        cuts = tuple(blocks[k].shape[4] // 2 for k in order)
+        small = jnp.zeros((16, norm_sum.shape[1]), jnp.float32)
+        small = small.at[:10].set(norm_sum).at[10, 0].set(loss_sum)
+        reduced = reduce_all([blocks[k] for k in order], cuts, small)
+        shares = [None] * 6
+        for k, value in zip(order, reduced):
+            shares[k] = value
+        norm_total = reduced[6][:10]
+        loss_total = reduced[6][10, 0]
+        square_total = reduced[6][11, 0]
+    else:
+        shares = [lax.psum_scatter(g, both, scatter_dimension=0, tiled=True) for g in local_grads]
+        squares = sum(jnp.sum(share * share) for share in shares)
+        norm_total, square_total, loss_total = lax.psum((norm_sum, squares, loss_sum), both)
+    grad_sum = (
+        jnp.stack([shares[0], shares[1]], axis=1),
+        jnp.stack([shares[2], shares[3]], axis=1),
+        shares[4],
+        shares[5].reshape(-1, code_width),
+    )
     grad_norm = jnp.sqrt(square_total + jnp.sum(norm_total * norm_total))
     factor = jnp.minimum(1.0, clip_level / grad_norm)
     grad_wide, grad_narrow, grad_edge, grad_book = grad_sum

time: 1990 us -> 624 us (0.31)
  waiting for transfers between devices: 1080 us -> 0.11 us
  Pallas kernels: 0 us -> 272 us
  matrix products: 372 us -> 182 us
  blocking collectives: 164 us -> 0 us
  other arithmetic: 201 us -> 88.8 us
  local copies, waits for them, and re-layouts: 117 us -> 52.4 us
    reduce_scatter x19 -> x4, waiting for transfers between devices: 783 us -> 0.05 us  [the longest x2 0.02 us: block_backward(): lax.psum_scatter(grad_values, 'band', scatter_dimension=0, tiled=True, ax...]
    pallas_call x0 -> x2, Pallas kernels: none -> 272 us  [the longest x1 160 us: reduce_all(): pl.pallas_call(functools.partial(reduce_kernel, cuts), out_shape=[jax.Sha...]
    all_gather x18 -> x0, waiting for transfers between devices: 169 us -> none  [the longest x8 116 us: block_forward(): lax.all_gather(projected[:, 2 * model_width:], 'band', axis=0, tiled=True)]
    unnamed x39 -> x4, waiting for transfers between devices: 126 us -> 0.07 us
    all_gather x2 -> x0, blocking collectives: 84.6 us -> none  [the longest x1 45.4 us: body(): lax.all_gather(shards[2], ('img', 'band'), axis=0, tiled=True)]
    another operation x32 -> x4, other arithmetic: 89.8 us -> 6.32 us  [the longest x8 43.3 us: micro_step(): jnp.stack([enc_wide, dec_wide], axis=1)]
    psum x2 -> x0, blocking collectives: 79.1 us -> none  [the longest x1 41.6 us: body(): lax.psum((norm_sum, squares, loss_sum), ('img', 'band'))]
    dot_general x48 -> x15, matrix products: 81.2 us -> 28.8 us  [matmul_outer(): lax.dot_general(first_op, second_op, (((0,), (0,)), ((), ())), preferred_...]
  transfers between devices with their start and end apart: 38 -> 4, of which waited for: 26 -> 0; matrix products, arithmetic and copies ran while one was open for 30% -> 20% of each run, Pallas kernels for 0% -> 0%
where the time goes in v1:
time: 624 us; the launch traced here: 617 us
  Pallas kernels  272 us (44%)
  matrix products  182 us (29%)
  other arithmetic  88.8 us (14%)
  local copies, waits for them, and re-layouts  52.4 us (8%)
  between operations  21.6 us (3%)
    pallas_call x1, Pallas kernels, reduce_all(): pl.pallas_call(functools.partial(reduce_kernel, cuts), out_shape=[jax.Sha...  160 us
    pallas_call x1, Pallas kernels, gather_all(): pl.pallas_call(functools.partial(gather_kernel, cuts), out_shape=out_shap...  112 us
    dot_general x16, matrix products, matmul_trans(): lax.dot_general(first_op, second_op, (((1,), (1,)), ((), ())), preferred_...  41.1 us
    dot_general x12, matrix products, matmul_plain(): return jnp.dot(first_op, second_op, preferred_element_type=jnp.float32)  31.4 us
    dot_general x15, matrix products, matmul_outer(): lax.dot_general(first_op, second_op, (((0,), (0,)), ((), ())), preferred_...  28.8 us
    unnamed x346, local copies, waits for them, and re-layouts  27.5 us
    dot_general x2, matrix products, attend_back(): jnp.einsum('qhd,khd->hqk', g_heads, v_heads, preferred_element_type=jnp.f...  23.3 us
    dot_general x2, matrix products, attend_back(): jnp.einsum('hqk,qhd->khd', softmaxed.astype(jnp.bfloat16), g_heads, prefe...  17.5 us
  transfers between devices with their start and end apart: 4, of which 0 were waited for; matrix products, arithmetic and copies ran while one was open for 20% of the time, Pallas kernels for 0%

profile of v1, /device:TPU:0, one launch (start us, length us, event | category | flops | bytes accessed | tf_op | source)
XLA Modules:
  0.0 616.8 jit_solution(9886903720246737166)
XLA Ops:
  20.3 112.2 %gather_all.1 = (bf16[4,2,2,2,64,128]{5,4,3,2,1,0:T(8,128)(2,1)}, bf16[4,2,2,2,16,448]{5,4,3,2,1,0:T(8,128)(2,1)}, bf16[4,2,2,2,112,512]{5,4,3,2,1,0:T(8,128)(2,...) custom-call(bf16[64,128]{1,0:T(8,128)(2,1)} %reshape.578.refs_0_, ...), custom_call_target="tpu_custom_call" | custom-call | tf_op jit(solution)/shard_map/gather_all/pallas_call | solution.py:401
  133.4 2.9 convolution_select_fusion
  139.1 3.2 convolution_convert_fusion.2
  147.2 5.1 fusion.228
  152.4 3.5 fusion
  158.3 3.8 fusion.73
  170.3 3.6 fusion.51
  189.0 6.7 %fusion.15 = bf16[512,2048]{1,0:T(8,128)(2,1)S(1)} fusion(f32[512,2048]{1,0:T(8,128)} %copy-done.156, bf16[2560,512]{1,0:T(8,128)(2,1)S(1)} %bitcast.285, f32[512,512]{0,1:T(8,128)S(1)} %get-tuple-element.149, f32[512]{0:T(512)S(1)} %negate_multiply_fusion.4), kind=kOutput, calls=%fused_computation.38 | convolution fusion | flops 1099431936 | bytes 9439232 | tf_op jit(solution)/shard_map/dot_general | solution.py:33
  208.2 8.7 %fusion.6 = f32[8,64,1024]{2,1,0:T(8,128)} fusion(bf16[512,8,64]{0,2,1:T(8,128)(2,1)S(1)} %bitcast.252, f32[8,512,1024]{2,1,0:T(8,128)} %copy-done.2, f32[8,512]{1,0:T(8,128)S(1)} %log_add_fusion.1), kind=kOutput, calls=%fused_computation.17 | convolution fusion | flops 545259520 | bytes 19415040 | tf_op jit(solution)/shard_map/hqk,qhd->khd/dot_general | solution.py:100
  216.9 9.0 %multiply_reduce_fusion.1 = (f32[8,512]{1,0:T(8,128)S(1)}, f32[8,512,1024]{2,1,0:T(8,128)S(1)}) fusion(f32[8,512,1024]{2,1,0:T(8,128)} %copy-done.2, f32[8,512]{1,0:T(8,128)S(1)} %log_add_fusion.1, bf16[512,8,64]{0,2,1:T(8,128)(2,1)S(1)} %bitcast.253, bf16[1024,8,64]{0,2,1:T(8,128)(2,1)} %bitcast.267), kind=kOutput, calls=%fused_computation.7 | convolution fusion | flops 549449728 | bytes 35160064 | tf_op jit(solution)/shard_map/qhd,khd->hqk/dot_general | solution.py:90
  226.0 7.8 %multiply_convert_fusion.1 = bf16[8,512,1024]{2,1,0:T(8,128)(2,1)S(1)} fusion(f32[8,512,1024]{2,1,0:T(8,128)S(1)} %get-tuple-element.193, f32[8,512,1024]{2,1,0:T(8,128)} %copy-done.2, f32[8,512]{1,0:T(8,128)S(1)} %get-tuple-element.192, f32[8,512]{1,0:T(8,128)S(1)} %log_add_fusion.1), kind=kLoop, calls=%fused_computation.6 | loop fusion | flops 16777216 | bytes 41975808 | tf_op jit(solution)/shard_map/convert_element_type | solution.py:92
  233.8 3.5 convolution_multiply_fusion.1
  246.4 3.2 fusion.232
  249.6 3.8 fusion.1
  255.4 3.8 fusion.72
  277.3 3.9 fusion.159
  288.3 4.2 fusion.236
  303.7 7.1 %fusion.19 = bf16[512,2048]{1,0:T(8,128)(2,1)} fusion(f32[512,2048]{1,0:T(8,128)} %copy-done.154, bf16[2560,512]{1,0:T(8,128)(2,1)S(1)} %bitcast.281, f32[512,512]{1,0:T(8,128)S(1)} %fusion.162), kind=kOutput, calls=%fused_computation.42 | convolution fusion | flops 1099169792 | bytes 9437184 | tf_op jit(solution)/shard_map/dot_general | solution.py:33
  313.3 5.0 fusion.235
  328.7 8.8 %fusion.4 = f32[8,64,1024]{2,1,0:T(8,128)} fusion(bf16[512,8,64]{0,2,1:T(8,128)(2,1)S(1)} %bitcast.250, f32[8,512,1024]{2,1,0:T(8,128)} %copy-done.1, f32[8,512]{1,0:T(8,128)S(1)} %log_add_fusion), kind=kOutput, calls=%fused_computation.16 | convolution fusion | flops 545259520 | bytes 19415040 | tf_op jit(solution)/shard_map/hqk,qhd->khd/dot_general | solution.py:100
  338.3 5.6 fusion.217
  344.0 14.3 %multiply_reduce_fusion = (f32[8,512]{1,0:T(8,128)S(1)}, f32[8,512,1024]{2,1,0:T(8,128)}) fusion(f32[8,512,1024]{2,1,0:T(8,128)} %copy-done.1, f32[8,512]{1,0:T(8,128)S(1)} %log_add_fusion, bf16[512,8,64]{0,2,1:T(8,128)(2,1)S(1)} %bitcast.251, bf16[1024,8,64]{0,2,1:T(8,128)(2,1)} %bitcast.266), kind=kOutput, calls=%fused_computation.1 | convolution fusion | flops 549449728 | bytes 35160064 | tf_op jit(solution)/shard_map/qhd,khd->hqk/dot_general | solution.py:90
  359.7 8.0 %multiply_convert_fusion = bf16[8,512,1024]{2,1,0:T(8,128)(2,1)S(1)} fusion(f32[8,512,1024]{2,1,0:T(8,128)} %get-tuple-element.201, f32[8,512,1024]{2,1,0:T(8,128)S(1)} %bitcast.224, f32[8,512]{1,0:T(8,128)S(1)} %get-tuple-element.200, f32[8,512]{1,0:T(8,128)S(1)} %log_add_fusion), kind=kLoop, calls=%fused_computation | loop fusion | flops 16777216 | bytes 41975808 | tf_op jit(solution)/shard_map/convert_element_type | solution.py:92
  367.8 3.5 convolution_multiply_fusion
  373.8 5.2 pad_maximum_fusion.2
  383.9 3.7 fusion.218
  389.4 2.9 pad_maximum_fusion.3
  395.0 3.8 pad_maximum_fusion
  404.3 4.3 fusion.234
  417.1 7.0 %pad_maximum_fusion.1 = f32[3584,512]{1,0:T(8,128)} fusion(f32[2048,512]{1,0:T(8,128)} %fusion.218, f32[1536,512]{1,0:T(8,128)} %fusion.109), kind=kLoop, calls=%fused_computation.24 | loop fusion | flops 1835008 | bytes 14680064 | tf_op jit(solution)/shard_map/concatenate | solution.py:161
  425.0 159.6 %reduce_all.1 = (f32[112,512]{1,0:T(8,128)}, f32[80,512]{1,0:T(8,128)}, f32[112,512]{1,0:T(8,128)}, f32[80,512]{1,0:T(8,128)}, f32[16,448]{1,0:T(8,128)}, /*index=5*/f32[64,128]{1,0:T(8,128)}, f32[16,512]{1,0:T(8,128)}) custom-call(f32[4,2,2,2,112,512]{5,4,3,2,1,0:T(8,128)} %bitcast.229, f32[4,2,2,2,80,512]{5,4,3,2,1,0:T(8,128)} %bitcast.231, ...), custom_call_target="tpu_custom_call" | custom-call | tf_op jit(solution)/shard_map/reduce_all/pallas_call | solution.py:554
  588.7 3.4 fusion.127
  (493 shorter events, 164.2 us)
Async XLA Ops:
  7.2 595.1 %copy-start = (f32[448,448]{1,0:T(8,128)S(1)}, f32[448,448]{1,0:T(8,128)}, u32[]{:S(2)}) copy-start(f32[448,448]{1,0:T(8,128)} %param.35) | copy-start | bytes 2408452
  7.2 9.6 %copy-start.85 = (bf16[4,1,128,192]{2,3,1,0:T(8,128)(2,1)S(1)}, bf16[4,1,128,192]{2,3,1,0:T(8,128)(2,1)}, u32[]{:S(2)}) copy-start(bf16[4,1,128,192]{2,3,1,0:T(8,128)(2,1)} %param.25) | copy-start | bytes 589828
  7.2 9.7 %copy-start.153 = (s32[4,1]{0,1:T(1,128)S(1)}, s32[4,1]{0,1:T(1,128)}, u32[]{:S(2)}) copy-start(s32[4,1]{0,1:T(1,128)} %param.28) | copy-start | bytes 52
  7.2 276.7 %reduce-scatter.7.cloned.1.call-start = ((), (), s32[]{:S(2)}) async-start(), calls=%async_computation.5 | async-start | bytes 3145728 | tf_op jit(solution)/shard_map/reduce_scatter | solution.py:151
  10.3 126.1 %copy-start.149 = (s32[128]{0:T(128)}, s32[128]{0:T(128)S(1)}, u32[]{:S(2)}) copy-start(s32[128]{0:T(128)S(1)} %and_select_fusion) | copy-start | bytes 1540
  19.1 117.3 %copy-start.100 = (f32[10,512]{1,0:T(8,128)S(1)}, f32[10,512]{1,0:T(8,128)}, u32[]{:S(2)}) copy-start(f32[10,512]{1,0:T(8,128)} %param.33) | copy-start | bytes 61444
  138.5 23.7 %copy-start.7 = (f32[1024,512]{0,1:T(8,128)}, f32[1024,512]{0,1:T(8,128)S(1)}, u32[]{:S(2)}) copy-start(f32[1024,512]{0,1:T(8,128)S(1)} %get-tuple-element.185) | copy-start | bytes 6291460
  216.9 69.3 %reduce-scatter.5.cloned.1.call-start = ((), (), s32[]{:S(2)}) async-start(), calls=%async_computation.4 | async-start | bytes 3145728 | tf_op jit(solution)/shard_map/reduce_scatter | solution.py:150
  237.8 161.1 %reduce-scatter.11.cloned.1.call-start = ((), (), s32[]{:S(2)}) async-start(), calls=%async_computation.7 | async-start | bytes 3145728 | tf_op jit(solution)/shard_map/reduce_scatter | solution.py:151
  239.6 98.0 %copy-start.5 = (f32[1024,512]{0,1:T(8,128)}, f32[1024,512]{0,1:T(8,128)S(1)}, u32[]{:S(2)}) copy-start(f32[1024,512]{0,1:T(8,128)S(1)} %get-tuple-element.195) | copy-start | bytes 6291460
  240.3 9.3 %copy-start.64 = (bf16[1024,512]{0,1:T(8,128)(2,1)}, bf16[1024,512]{0,1:T(8,128)(2,1)S(1)}, u32[]{:S(2)}) copy-start(bf16[1024,512]{0,1:T(8,128)(2,1)S(1)} %add_convert_fusion) | copy-start | bytes 3145732
  242.5 10.9 %copy-start.60 = (bf16[1024,512]{0,1:T(8,128)(2,1)}, bf16[1024,512]{0,1:T(8,128)(2,1)S(1)}, u32[]{:S(2)}) copy-start(bf16[1024,512]{0,1:T(8,128)(2,1)S(1)} %convolution_convert_fusion) | copy-start | bytes 3145732
  283.9 8.6 %copy-start.70 = (bf16[8,64,512]{2,1,0:T(8,128)(2,1)}, bf16[8,64,512]{2,1,0:T(8,128)(2,1)S(1)}, u32[]{:S(2)}) copy-start(bf16[8,64,512]{2,1,0:T(8,128)(2,1)S(1)} %fusion.67) | copy-start | bytes 1572868
  328.7 8.9 %copy-start.39 = (bf16[512,512]{0,1:T(8,128)(2,1)}, bf16[512,512]{0,1:T(8,128)(2,1)S(1)}, u32[]{:S(2)}) copy-start(bf16[512,512]{0,1:T(8,128)(2,1)S(1)} %convolution_convert_fusion.4) | copy-start | bytes 1572868
  337.6 62.6 %reduce-scatter.9.cloned.1.call-start = ((), (), s32[]{:S(2)}) async-start(), calls=%async_computation.6 | async-start | bytes 3145728 | tf_op jit(solution)/shard_map/reduce_scatter | solution.py:150
  338.3 19.9 %slice-start = ((s8[16777216]{0:T(1024)(128)(4,1)}), s8[4194304]{0:T(1024)(128)(4,1)S(1)}, s32[]{:S(2)}) async-start(s8[16777216]{0:T(1024)(128)(4,1)} %bitcast.223), calls=%async_computation.8 | async-start | bytes 8388608
  344.0 14.3 %slice-start.1 = ((s8[16777216]{0:T(1024)(128)(4,1)}), s8[4194304]{0:T(1024)(128)(4,1)S(1)}, s32[]{:S(2)}) async-start(s8[16777216]{0:T(1024)(128)(4,1)} %bitcast.223), calls=%async_computation.9 | async-start | bytes 8388608
  344.0 14.3 %slice-start.2 = ((s8[16777216]{0:T(1024)(128)(4,1)}), s8[4194304]{0:T(1024)(128)(4,1)S(1)}, s32[]{:S(2)}) async-start(s8[16777216]{0:T(1024)(128)(4,1)} %bitcast.223), calls=%async_computation.10 | async-start | bytes 8388608
  344.0 15.8 %slice-start.3 = ((s8[16777216]{0:T(1024)(128)(4,1)}), s8[4194304]{0:T(1024)(128)(4,1)S(1)}, s32[]{:S(2)}) async-start(s8[16777216]{0:T(1024)(128)(4,1)} %bitcast.223), calls=%async_computation.11 | async-start | bytes 8388608
  359.7 8.0 %copy-start.36 = (bf16[512,512]{0,1:T(8,128)(2,1)S(1)}, bf16[512,512]{0,1:T(8,128)(2,1)}, u32[]{:S(2)}) copy-start(bf16[512,512]{0,1:T(8,128)(2,1)} %copy-done.35) | copy-start | bytes 1572868
  383.9 8.5 %slice-start.6 = ((s8[8388608]{0:T(1024)(128)(4,1)}), s8[4194304]{0:T(1024)(128)(4,1)S(1)}, s32[]{:S(2)}) async-start(s8[8388608]{0:T(1024)(128)(4,1)} %bitcast.227), calls=%async_computation.14 | async-start | bytes 8388608
  425.0 163.7 %copy-start.76 = (f32[112,2,512]{2,1,0:T(2,128)S(1)}, f32[112,2,512]{2,1,0:T(2,128)}, u32[]{:S(2)}) copy-start(f32[112,2,512]{2,1,0:T(2,128)} %param.37) | copy-start | bytes 1376260
  425.0 163.7 %copy-start.77 = (f32[112,2,512]{2,1,0:T(2,128)S(1)}, f32[112,2,512]{2,1,0:T(2,128)}, u32[]{:S(2)}) copy-start(f32[112,2,512]{2,1,0:T(2,128)} %param.36) | copy-start | bytes 1376260
  584.6 8.6 %copy-start.57 = (f32[112,2,512]{2,1,0:T(2,128)S(1)}, f32[112,2,512]{2,1,0:T(2,128)}, u32[]{:S(2)}) copy-start(f32[112,2,512]{2,1,0:T(2,128)} %param.29) | copy-start | bytes 1376260
  598.1 9.0 %copy-start.114 = (f32[64,128]{1,0:T(8,128)S(1)}, f32[64,128]{1,0:T(8,128)}, u32[]{:S(2)}) copy-start(f32[64,128]{1,0:T(8,128)} %get-tuple-element.72) | copy-start | bytes 98308
  599.1 8.2 %copy-start.90 = (f32[16,512]{1,0:T(8,128)S(1)}, f32[16,512]{1,0:T(8,128)}, u32[]{:S(2)}) copy-start(f32[16,512]{1,0:T(8,128)} %get-tuple-element.66) | copy-start | bytes 98308
  599.1 8.2 %copy-start.101 = (f32[10,512]{1,0:T(8,128)S(1)}, f32[10,512]{1,0:T(8,128)}, u32[]{:S(2)}) copy-start(f32[10,512]{1,0:T(8,128)} %param.33) | copy-start | bytes 61444
  599.1 8.2 %copy-start.109 = (f32[10,512]{1,0:T(8,128)S(1)}, f32[10,512]{1,0:T(8,128)}, u32[]{:S(2)}) copy-start(f32[10,512]{1,0:T(8,128)} %param.45) | copy-start | bytes 61444
  599.1 8.2 %copy-start.110 = (f32[10,512]{1,0:T(8,128)S(1)}, f32[10,512]{1,0:T(8,128)}, u32[]{:S(2)}) copy-start(f32[10,512]{1,0:T(8,128)} %param.44) | copy-start | bytes 61444
  599.1 8.9 %copy-start.95 = (f32[256,32]{0,1:T(8,128)S(1)}, f32[256,32]{0,1:T(8,128)}, u32[]{:S(2)}) copy-start(f32[256,32]{0,1:T(8,128)} %param.32) | copy-start | bytes 98308
  599.1 8.9 %copy-start.111 = (f32[256,32]{0,1:T(8,128)S(1)}, f32[256,32]{0,1:T(8,128)}, u32[]{:S(2)}) copy-start(f32[256,32]{0,1:T(8,128)} %param.43) | copy-start | bytes 98308
  599.2 8.9 %copy-start.112 = (f32[256,32]{0,1:T(8,128)S(1)}, f32[256,32]{0,1:T(8,128)}, u32[]{:S(2)}) copy-start(f32[256,32]{0,1:T(8,128)} %param.42) | copy-start | bytes 98308
  (138 other events, 610.9 us)
Sparse Core Ops, SparseCore 0:
  217.0 8.0 reduce-scatter.6
  237.9 7.7 reduce-scatter.4
  337.7 7.7 reduce-scatter.10
  371.9 8.5 reduce-scatter.8

commit v2 on v1

--- a/solution.py
+++ b/solution.py
@@ -415,6 +415,380 @@
         compiler_params=pltpu.CompilerParams(collective_id=0, has_side_effects=True),
         name="gather_all",
     )(*shards, slab, code, tally)
+
+
+def dot_nn(a, b):
+    return lax.dot_general(a, b, (((1,), (0,)), ((), ())), preferred_element_type=jnp.float32)
+
+
+def dot_nt(a, b):
+    return lax.dot_general(a, b, (((1,), (1,)), ((), ())), preferred_element_type=jnp.float32)
+
+
+def dot_tn(a, b):
+    return lax.dot_general(a, b, (((0,), (0,)), ((), ())), preferred_element_type=jnp.float32)
+
+
+def norm_parts(h):
+    centred = h - jnp.mean(h, axis=-1, keepdims=True)
+    rate = lax.rsqrt(jnp.mean(centred * centred, axis=-1, keepdims=True) + norm_eps)
+    return centred * rate, rate
+
+
+def norm_back(grad, h, gain):
+    shape, rate = norm_parts(h)
+    inner = grad * gain
+    back = rate * (
+        inner
+        - jnp.mean(inner, axis=-1, keepdims=True)
+        - shape * jnp.mean(inner * shape, axis=-1, keepdims=True)
+    )
+    return (
+        back,
+        jnp.sum(grad * shape, axis=0, keepdims=True),
+        jnp.sum(grad, axis=0, keepdims=True),
+    )
+
+
+STEP = 256
+
+
+def block_kernel(decoder, latent_total, *refs):
+    n_in = 12 if decoder else 13
+    if decoder:
+        (code_col, book, first_w, wide, narrow, norms, q_extra, k_extra, e_pix, pix_own, mask_own, tally) = refs[:n_in]
+        (g_wide, g_narrow, small, g_head, g_first, chosen_out, cross_out) = refs[n_in : n_in + 7]
+        rest = refs[n_in + 7 :]
+    else:
+        (source, first_w, wide, narrow, norms, q_extra, k_extra, e_qin, pix_own, chosen, cross, code_col, code_row) = refs[:n_in]
+        (g_wide, g_narrow, small, g_head, g_first, g_book) = refs[n_in : n_in + 6]
+        rest = refs[n_in + 6 :]
+    (hidden, normed, q_buf, kv, probs, att, middle, second, slope, active, grad_out, grad_low, gup, gatt,
+     dkv, dkv_in, dqkv, stage, stage_sem, x_send, x_recv) = rest[:21]
+    if decoder:
+        spread, = rest[21:22]
+        source = spread
+    img_at, band_at, y_at, x_at, part = place()
+    barrier = pltpu.get_barrier_semaphore()
+    sibling = (img_at, band_at + 1 - 2 * part)
+    pl.semaphore_signal(barrier, inc=1, device_id=sibling, device_id_type=MESH)
+    pl.semaphore_wait(barrier, 1)
+    total_rows, width = hidden.shape
+    own_rows = q_buf.shape[0]
+    own = pl.multiple_of(part * own_rows, own_rows)
+    base = 4 if decoder else 0
+    chunks_all, chunks_own = total_rows // STEP, own_rows // STEP
+    f32, bf16 = jnp.float32, jnp.bfloat16
+
+    def at(k):
+        return pl.ds(pl.multiple_of(k * STEP, STEP), STEP)
+
+    def at_own(k):
+        return pl.ds(pl.multiple_of(own + k * STEP, STEP), STEP)
+
+    def gain(k):
+        return norms[pl.ds(base + k, 1), :]
+
+    small[...] = jnp.zeros(small.shape, f32)
+
+    def enter(k, carry):
+        rows = at(k)
+        if decoder:
+            code = code_col[rows]
+            fold = book.shape[1] // 32
+            picks = lax.broadcasted_iota(jnp.int32, (STEP, book.shape[0]), 1)
+            hot = jnp.where(picks == code // fold, 1.0, 0.0).astype(bf16)
+            lanes = lax.broadcasted_iota(jnp.int32, (STEP, book.shape[1]), 1) // 32
+            spread[rows] = jnp.where(lanes == code % fold, dot_nn(hot, book[...]), 0.0).astype(bf16)
+        h = dot_nt(source[rows], first_w[...])
+        hidden[rows] = h
+        shape, _ = norm_parts(h)
+        low = (shape * gain(0) + gain(1)).astype(bf16)
+        normed[rows] = low
+        kv[rows] = dot_nt(low, wide[width : 3 * width]).astype(bf16)
+        return carry
+
+    lax.fori_loop(0, chunks_all, enter, 0)
+
+    def make_q(k, carry):
+        q_buf[at(k)] = (dot_nt(normed[at_own(k)], wide[:width]).astype(bf16).astype(f32) * HDIM**-0.5).astype(bf16)
+        return carry
+
+    lax.fori_loop(0, chunks_own, make_q, 0)
+    lane_head = lax.broadcasted_iota(jnp.int32, (1, 128), 1) // HDIM
+    picks_head = [jnp.where(lane_head == k, 1.0, 0.0).astype(bf16) for k in range(2)]
+
+    def pair_lanes(p, offset=0):
+        return pl.ds(pl.multiple_of(offset + p * 128, 128), 128)
+
+    def attend_pair(p, carry):
+        k_cat = jnp.concatenate([kv[:, pair_lanes(p)], k_extra[...]], axis=1)
+        v_pair = kv[:, pair_lanes(p, width)]
+
+        def rows_step(j, inner):
+            rows = at(j)
+            q_pair = q_buf[rows, pair_lanes(p)]
+            mixed = None
+            for k in range(2):
+                q_cat = jnp.concatenate([q_pair * picks_head[k], q_extra[rows]], axis=1)
+                scores = dot_nt(q_cat, k_cat)
+                expo = jnp.exp(scores - jnp.max(scores, axis=-1, keepdims=True))
+                prob = expo * (1.0 / jnp.sum(expo, axis=-1, keepdims=True))
+                probs[2 * p + k, rows] = prob
+                term = dot_nn(prob.astype(bf16), v_pair * picks_head[k])
+                mixed = term if mixed is None else mixed + term
+            att[rows, pair_lanes(p)] = mixed.astype(bf16)
+            return inner
+
+        return lax.fori_loop(0, chunks_own, rows_step, carry)
+
+    lax.fori_loop(0, width // 128, attend_pair, 0)
+
+    def after_attention(k, carry):
+        rows = at(k)
+        mid = hidden[at_own(k)] + dot_nn(att[rows], narrow[:width])
+        middle[rows] = mid
+        shape, _ = norm_parts(mid)
+        second[rows] = (shape * gain(2) + gain(3)).astype(bf16)
+        grad_out[rows] = mid
+        return carry
+
+    lax.fori_loop(0, chunks_own, after_attention, 0)
+
+    def mlp(n, carry):
+        f = n // chunks_own
+        rows = at(n % chunks_own)
+        feature = pl.ds(pl.multiple_of(f * width, width), width)
+        u = dot_nt(second[rows], wide[pl.ds(pl.multiple_of((3 + f) * width, width), width)])
+        squared = u * u
+        bend = jnp.tanh(0.7978845608028654 * (u + 0.044715 * squared * u))
+        low = (0.5 * u * (1.0 + bend)).astype(bf16)
+        active[rows, feature] = low
+        slope[rows, feature] = 0.5 * (1.0 + bend) + (0.5 * u) * (1.0 - bend * bend) * (
+            0.7978845608028654 * (1.0 + (3.0 * 0.044715) * squared)
+        )
+        grad_out[rows] += dot_nn(low, narrow[pl.ds(pl.multiple_of((1 + f) * width, width), width)])
+        return carry
+
+    lax.fori_loop(0, 4 * chunks_own, mlp, 0)
+
+    def add_small(row, value):
+        small[pl.ds(row, 1), :] += value
+
+    first_lane = lax.broadcasted_iota(jnp.int32, (1, width), 1) == 0
+
+    def add_loss(value):
+        add_small(6, jnp.where(first_lane, value, 0.0))
+
+    def head(k, carry):
+        rows = at(k)
+        out = grad_out[rows]
+        if decoder:
+            shape, _ = norm_parts(out)
+            final = (shape * norms[pl.ds(8, 1), :] + norms[pl.ds(9, 1), :]).astype(bf16)
+            error = dot_nn(final, e_pix[...]) - pix_own[rows].astype(f32)
+            counted = mask_own[rows].astype(f32)
+            number = tally[0:1, 0:1]
+            add_loss(jnp.sum(counted * (error * error + jnp.abs(error))) / number)
+            sign = jnp.where(error > 0.0, 1.0, jnp.where(error < 0.0, -1.0, 0.0))
+            grad_pred = (counted * (2.0 * error + sign) / number).astype(bf16)
+            g_head[...] += dot_tn(final, grad_pred)
+            back, g_gain, g_offset = norm_back(dot_nt(grad_pred, e_pix[...]), out, norms[pl.ds(8, 1), :])
+            add_small(4, g_gain)
+            add_small(5, g_offset)
+        else:
+            low = out.astype(bf16)
+            lanes = lax.broadcasted_iota(jnp.int32, (STEP, 128), 1) // 32
+            mine = lanes == code_col[at_own(k)] % 4
+            gap = jnp.where(mine, chosen[rows].astype(f32) - dot_nn(low, e_qin[...]), 0.0)
+            add_loss((1.0 + commitment) * jnp.sum(gap * gap) / latent_total)
+            grad_latent = jnp.where(mine, cross[rows] - 2.0 * commitment * gap / latent_total, 0.0).astype(bf16)
+            g_head[...] += dot_tn(low, grad_latent)
+            back = dot_nt(grad_latent, e_qin[...])
+            gap = 2.0 * gap / latent_total
+            high = gap.astype(bf16)
+            left = gap - high.astype(f32)
+            between = left.astype(bf16)
+            parts = jnp.concatenate([high, between, (left - between.astype(f32)).astype(bf16)], axis=1)
+            split[rows] = parts
+        grad_out[rows] = back
+        grad_low[rows] = back.astype(bf16)
+        return carry
+
+    g_head[...] = jnp.zeros(g_head.shape, f32)
+    if not decoder:
+        split = rest[21]
+    lax.fori_loop(0, chunks_own, head, 0)
+
+    if not decoder:
+        def book_rows(k, carry):
+            picks = lax.broadcasted_iota(jnp.int32, (STEP, own_rows), 0) + k * STEP
+            hot = jnp.where(picks == code_row[...] // 4, 1.0, 0.0).astype(bf16)
+            summed = dot_nn(hot, split[...])
+            g_book[at(k)] = (summed[:, :128] + summed[:, 128:256]) + summed[:, 256:]
+            return carry
+        lax.fori_loop(0, g_book.shape[0] // STEP, book_rows, 0)
+
+    def mlp_back(k, carry):
+        rows = at(k)
+        gy = grad_low[rows]
+
+        def feature_step(f, acc):
+            feature = pl.ds(pl.multiple_of(f * width, width), width)
+            ga = dot_nt(gy, narrow[pl.ds(pl.multiple_of((1 + f) * width, width), width)])
+            low = (ga * slope[rows, feature]).astype(bf16)
+            gup[rows, feature] = low
+            return acc + dot_nn(low, wide[pl.ds(pl.multiple_of((3 + f) * width, width), width)])
+
+        gsec = lax.fori_loop(0, 4, feature_step, jnp.zeros((STEP, width), f32))
+        back, g_gain, g_offset = norm_back(gsec, middle[rows], gain(2))
+        add_small(2, g_gain)
+        add_small(3, g_offset)
+        grad_mid = back + grad_out[rows]
+        grad_out[rows] = grad_mid
+        low = grad_mid.astype(bf16)
+        mid_low[rows] = low
+        gatt[rows] = dot_nt(low, narrow[:width]).astype(bf16)
+        return carry
+
+    mid_low = rest[22]
+    lax.fori_loop(0, chunks_own, mlp_back, 0)
+
+    def attend_back_pair(p, carry):
+        k_pair = kv[:, pair_lanes(p)]
+        v_pair = kv[:, pair_lanes(p, width)]
+        dkv[:, pair_lanes(p)] = jnp.zeros((total_rows, 128), f32)
+        dkv[:, pair_lanes(p, width)] = jnp.zeros((total_rows, 128), f32)
+
+        def rows_step(j, inner):
+            rows = at(j)
+            q_pair = q_buf[rows, pair_lanes(p)]
+            g_pair = gatt[rows, pair_lanes(p)]
+            dq = None
+            for k in range(2):
+                g_head_rows = g_pair * picks_head[k]
+                prob = probs[2 * p + k, rows]
+                d_prob = dot_nt(g_head_rows, v_pair)
+                dot_row = jnp.sum(prob * d_prob, axis=-1, keepdims=True)
+                d_score = (prob * (d_prob - dot_row)).astype(bf16)
+                term = dot_nn(d_score, k_pair * picks_head[k])
+                dq = term if dq is None else dq + term
+                dkv[:, pair_lanes(p)] += dot_tn(d_score, q_pair * picks_head[k])
+                dkv[:, pair_lanes(p, width)] += dot_tn(prob.astype(bf16), g_head_rows)
+            dqkv[rows, pair_lanes(p)] = (dq * HDIM**-0.5).astype(bf16)
+            return inner
+
+        return lax.fori_loop(0, chunks_own, rows_step, carry)
+
+    lax.fori_loop(0, width // 128, attend_back_pair, 0)
+    theirs = pl.ds(pl.multiple_of((1 - part) * own_rows, own_rows), own_rows)
+    swap = far_copy(dkv.at[theirs], dkv_in, x_send, x_recv, sibling)
+    swap.start()
+
+    def emit(lhs, rhs, rhs_rows, out, out_row, count):
+        def copy_of(k):
+            slot = k % 2
+            return pltpu.make_async_copy(
+                stage.at[slot], out.at[pl.ds(pl.multiple_of((out_row + k) * width, width), width)], stage_sem.at[slot]
+            )
+
+        def step(k, carry):
+            value = dot_tn(lhs[:, pl.ds(pl.multiple_of(k * width, width), width)], rhs[rhs_rows])
+
+            @pl.when(k >= 2)
+            def _():
+                copy_of(k - 2).wait()
+
+            stage[k % 2] = value
+            copy_of(k).start()
+            return carry
+
+        lax.fori_loop(0, count, step, 0)
+        for k in range(max(0, count - 2), count):
+            copy_of(k).wait()
+
+    every = slice(None)
+    emit(active, grad_low, every, g_narrow, 1, 4)
+    emit(gup, second, every, g_wide, 3, 4)
+    emit(att, mid_low, every, g_narrow, 0, 1)
+    swap.wait()
+
+    def join(k, carry):
+        rows = at(k)
+        dqkv[rows, width:] = (dkv[at_own(k)] + dkv_in[rows]).astype(bf16)
+        return carry
+
+    lax.fori_loop(0, chunks_own, join, 0)
+    emit(dqkv, normed, pl.ds(own, own_rows), g_wide, 0, 3)
+    g_first[...] = jnp.zeros(g_first.shape, f32)
+
+    def leave(k, carry):
+        rows = at(k)
+        grad_normed = dot_nn(dqkv[rows], wide[: 3 * width])
+        back, g_gain, g_offset = norm_back(grad_normed, hidden[at_own(k)], gain(0))
+        add_small(0, g_gain)
+        add_small(1, g_offset)
+        low = (back + grad_out[rows]).astype(bf16)
+        if decoder:
+            mine = spread[at_own(k)]
+            chosen_out[rows] = mine
+            cross_out[rows] = dot_nn(low, first_w[...])
+            g_first[...] += dot_tn(low, mine)
+        else:
+            g_first[...] += dot_tn(low, pix_own[rows])
+        return carry
+
+    lax.fori_loop(0, chunks_own, leave, 0)
+
+
+def run_block(decoder, latent_total, inputs, total_rows, own_rows):
+    width = 512
+    f32, bf16 = jnp.float32, jnp.bfloat16
+    any_space = pl.BlockSpec(memory_space=pl.ANY)
+    vmem = pl.BlockSpec(memory_space=pltpu.VMEM)
+    shape = jax.ShapeDtypeStruct
+    out_shape = [shape((7 * width, width), f32), shape((5 * width, width), f32), shape((8, width), f32)]
+    if decoder:
+        out_shape += [shape((width, 192), f32), shape((width, 128), f32)]
+        out_shape += [shape((own_rows, 128), bf16), shape((own_rows, 128), f32)]
+    else:
+        out_shape += [shape((width, 128), f32), shape((width, 192), f32), shape((2048, 128), f32)]
+    scratch = [
+        pltpu.VMEM((total_rows, width), f32),
+        pltpu.VMEM((total_rows, width), bf16),
+        pltpu.VMEM((own_rows, width), bf16),
+        pltpu.VMEM((total_rows, 2 * width), bf16),
+        pltpu.VMEM((HEADS, own_rows, total_rows), f32),
+        pltpu.VMEM((own_rows, width), bf16),
+        pltpu.VMEM((own_rows, width), f32),
+        pltpu.VMEM((own_rows, width), bf16),
+        pltpu.VMEM((own_rows, 4 * width), f32),
+        pltpu.VMEM((own_rows, 4 * width), bf16),
+        pltpu.VMEM((own_rows, width), f32),
+        pltpu.VMEM((own_rows, width), bf16),
+        pltpu.VMEM((own_rows, 4 * width), bf16),
+        pltpu.VMEM((own_rows, width), bf16),
+        pltpu.VMEM((total_rows, 2 * width), f32),
+        pltpu.VMEM((own_rows, 2 * width), f32),
+        pltpu.VMEM((own_rows, 3 * width), bf16),
+        pltpu.VMEM((2, width, width), f32),
+        pltpu.SemaphoreType.DMA((2,)),
+        pltpu.SemaphoreType.DMA,
+        pltpu.SemaphoreType.DMA,
+        pltpu.VMEM((total_rows, 128), bf16) if decoder else pltpu.VMEM((own_rows, 384), bf16),
+        pltpu.VMEM((own_rows, width), bf16),
+    ]
+    return pl.pallas_call(
+        functools.partial(block_kernel, decoder, latent_total),
+        out_shape=out_shape,
+        in_specs=[vmem] * len(inputs),
+        out_specs=[any_space] * 2 + [vmem] * (len(out_shape) - 2),
+        scratch_shapes=scratch,
+        compiler_params=pltpu.CompilerParams(
+            collective_id=2 if decoder else 3, has_side_effects=True, vmem_limit_bytes=60 << 20
+        ),
+        name="decoder_step" if decoder else "encoder_step",
+    )(*inputs)
 
 
 def reduce_kernel(cuts, *refs):
@@ -647,17 +1021,60 @@
 
         slab_all = whole_row(slab)
         code_all = whole_row(codes[:, 0])
-    gathered = (wholes[:2], wholes[2:4], wholes[4], wholes[5])
-    pixel_all = slab_all[:, :patch_size]
-    valid_rows = lax.dynamic_slice_in_dim(slab_all, part * own_rows, own_rows, 0)[:, patch_size:]
-    positions = jnp.arange(length, dtype=jnp.int32)
-    own_positions = part * own_rows + jnp.arange(own_rows, dtype=jnp.int32)
     kind = lax.dynamic_index_in_dim(image_kind[:, 0], row, 0, keepdims=False)
     span = jnp.where(kind == 0, length, length // 4)
-    allowed = (own_positions // span)[:, None] == (positions // span)[None, :]
-    local_grads, norm_sum, loss_sum = row_step(
-        gathered, norms, pixel_all, valid_rows, code_all, part, allowed, count, latent_total, groups
-    )
+    positions = jnp.arange(length, dtype=jnp.int32)
+    if direct:
+        own = functools.partial(lax.dynamic_slice_in_dim, start_index=part * own_rows, slice_size=own_rows, axis=0)
+        edge_all = wholes[4]
+        pixel_all = slab_all[:, :patch_size]
+        slab_own = own(slab_all)
+        pix_own, mask_own = slab_own[:, :patch_size], slab_own[:, patch_size:]
+        edge_in = edge_all[:, :patch_size]
+        edge_pix = edge_all[:, patch_size : 2 * patch_size]
+        edge_qin = jnp.tile(edge_all[:, 2 * patch_size : 2 * patch_size + code_width], (1, 4))
+        edge_qout = jnp.tile(edge_all[:, 2 * patch_size + code_width :], (1, 4))
+        lanes = jnp.arange(128, dtype=jnp.int32)[None, :]
+        segment = (positions // span)[:, None]
+        k_extra = (lanes == segment).astype(jnp.bfloat16)
+        q_extra = own(jnp.where((lanes < 4) & (lanes != segment), -(2.0**30), 0.0).astype(jnp.bfloat16))
+        code_col = code_all[:, None]
+        dec = run_block(
+            True,
+            latent_total,
+            (code_col, wholes[5], edge_qout, wholes[1], wholes[3], norms, q_extra, k_extra, edge_pix, pix_own,
+             mask_own, moved[8]),
+            length,
+            own_rows,
+        )
+        enc = run_block(
+            False,
+            latent_total,
+            (pixel_all, edge_in, wholes[0], wholes[2], norms, q_extra, k_extra, edge_qin, pix_own, dec[5], dec[6],
+             code_col, own(code_all)[None, :]),
+            length,
+            own_rows,
+        )
+
+        def fold(g):
+            return sum(g[:, k * code_width : (k + 1) * code_width] for k in range(4))
+
+        local_grads = (
+            enc[0], dec[0], enc[1], dec[1],
+            jnp.concatenate([enc[4], dec[3], fold(enc[3]), fold(dec[4])], axis=1),
+            enc[5],
+        )
+        norm_sum = jnp.concatenate([enc[2][:4], dec[2][:6]], axis=0)
+        loss_sum = enc[2][6, 0] + dec[2][6, 0]
+    else:
+        gathered = (wholes[:2], wholes[2:4], wholes[4], wholes[5])
+        pixel_all = slab_all[:, :patch_size]
+        valid_rows = lax.dynamic_slice_in_dim(slab_all, part * own_rows, own_rows, 0)[:, patch_size:]
+        own_positions = part * own_rows + jnp.arange(own_rows, dtype=jnp.int32)
+        allowed = (own_positions // span)[:, None] == (positions // span)[None, :]
+        local_grads, norm_sum, loss_sum = row_step(
+            gathered, norms, pixel_all, valid_rows, code_all, part, allowed, count, latent_total, groups
+        )
     if direct:
         blocks = [g.reshape((4, 2, 2, 2, g.shape[0] // 32, g.shape[1])) for g in local_grads]
         order = (1, 3, 0, 2, 4, 5)

time: 624 us -> 464 us (0.74)
  matrix products: 182 us -> 12.4 us
  Pallas kernels: 272 us -> 404 us
  other arithmetic: 88.8 us -> 13.9 us
  local copies, waits for them, and re-layouts: 52.4 us -> 26.7 us
  between operations: 21.6 us -> 5.57 us
    dot_general x55 -> x0, matrix products: 170 us -> none  [the longest x16 41.1 us: matmul_trans(): lax.dot_general(first_op, second_op, (((1,), (1,)), ((), ())), preferred_...]
    pallas_call x0 -> x2, Pallas kernels: none -> 133 us  [run_block(): pl.pallas_call(functools.partial(block_kernel, decoder, latent_total), ou...]
    reduce_sum x19 -> x0, other arithmetic: 29.4 us -> none  [the longest x5 11.4 us: layer_norm(): return centred * lax.rsqrt(spread + norm_eps) * scale_gain + offset]
    convert_element_type x10 -> x2, other arithmetic: 19.1 us -> 1.7 us  [the longest x1 0.9 us: body(): k_extra = (lanes == segment).astype(jnp.bfloat16)]
    unnamed x346 -> x64, local copies, waits for them, and re-layouts: 27.5 us -> 10.9 us
    concatenate x5 -> x2, other arithmetic: 19 us -> 2.44 us  [the longest x1 2.43 us: body(): jnp.concatenate([enc[4], dec[3], fold(enc[3]), fold(dec[4])], axis=1)]
    dot_general x6 -> x0, local copies, waits for them, and re-layouts: 15.4 us -> none  [the longest x4 10.3 us: matmul_plain(): return jnp.dot(first_op, second_op, preferred_element_type=jnp.float32)]
    another operation x4 -> x0, other arithmetic: 6.32 us -> none
  transfers between devices with their start and end apart: 4 -> 0, of which waited for: 0 -> 0; matrix products, arithmetic and copies ran while one was open for 20% -> 0% of each run, Pallas kernels for 0% -> 0%
where the time goes in v2:
time: 464 us; the launch traced here: 463 us
  Pallas kernels  404 us (87%)
  local copies, waits for them, and re-layouts  26.7 us (6%)
  other arithmetic  13.9 us (3%)
  matrix products  12.4 us (3%)
  between operations  5.57 us (1%)
    pallas_call x1, Pallas kernels, reduce_all(): pl.pallas_call(functools.partial(reduce_kernel, cuts), out_shape=[jax.Sha...  159 us
    pallas_call x2, Pallas kernels, run_block(): pl.pallas_call(functools.partial(block_kernel, decoder, latent_total), ou...  133 us
    pallas_call x1, Pallas kernels, gather_all(): pl.pallas_call(functools.partial(gather_kernel, cuts), out_shape=out_shap...  112 us
    unnamed x64, local copies, waits for them, and re-layouts  10.9 us

profile of v2, /device:TPU:0, one launch (start us, length us, event | category | flops | bytes accessed | tf_op | source)
XLA Modules:
  0.0 463.0 jit_solution(8483696974138348391)
XLA Ops:
  0.7 1.2 copy.136
  2.6 1.0 copy.137
  4.3 1.2 copy.96
  5.6 1.1 copy.95
  6.6 0.9 pad_maximum_fusion.1.refs_6_
  9.7 1.2 broadcast_in_dim.26.refs_8_
  10.9 112.3 %gather_all.1 = (bf16[4,2,2,2,64,128]{5,4,3,2,1,0:T(8,128)(2,1)}, bf16[4,2,2,2,16,448]{5,4,3,2,1,0:T(8,128)(2,1)}, bf16[4,2,2,2,112,512]{5,4,3,2,1,0:T(8,128)(2,...) custom-call(bf16[64,128]{1,0:T(8,128)(2,1)} %reshape.192.refs_0_, ...), custom_call_target="tpu_custom_call" | custom-call | tf_op jit(solution)/shard_map/gather_all/pallas_call | solution.py:401
  123.2 2.4 fusion.88
  127.9 0.9 fusion.42.refs_7_.refs_6_
  128.8 1.1 fusion.89
  130.7 1.7 copy.98.refs_0_.refs_11_
  132.4 66.4 %decoder_step.1 = (f32[3584,512]{1,0:T(8,128)}, f32[2560,512]{1,0:T(8,128)}, f32[8,512]{1,0:T(8,128)}, f32[512,192]{1,0:T(8,128)}, f32[512,128]{1,0:T(8,128)}, /...) custom-call(s32[1024,1]{1,0:T(8,128)} %copy.98.refs_0_.refs_11_, bf16[2048,128]{1,0:T(8,128)(2,1)} %bitcast.125, ...), custom_call_target="tpu_custom_call" | custom-call | tf_op jit(solution)/shard_map/decoder_step/pallas_call | solution.py:781
  201.2 66.5 %encoder_step.1 = (f32[3584,512]{1,0:T(8,128)}, f32[2560,512]{1,0:T(8,128)}, f32[8,512]{1,0:T(8,128)}, f32[512,128]{1,0:T(8,128)}, f32[512,192]{1,0:T(8,128)}, /*index=5*/f32[2048,128]{1,0:T(8,128)}) custom-call(bf16[1024,192]{1,0:T(8,128)(2,1)} %slice.157.refs_0_, bf16[512,192]{1,0:T(8,128)(2,1)} %get-tuple-element.175.refs_1_, ...), custom_call_target="tpu_custom_call" | custom-call | tf_op jit(solution)/shard_map/encoder_step/pallas_call | solution.py:781
  267.7 1.2 slice.144
  271.6 1.7 slice_add_fusion.1
  273.6 2.4 pad_maximum_fusion
  276.1 159.2 %reduce_all.1 = (f32[112,512]{1,0:T(8,128)}, f32[80,512]{1,0:T(8,128)}, f32[112,512]{1,0:T(8,128)}, f32[80,512]{1,0:T(8,128)}, f32[16,448]{1,0:T(8,128)}, /*index=5*/f32[64,128]{1,0:T(8,128)}, f32[16,512]{1,0:T(8,128)}) custom-call(f32[4,2,2,2,112,512]{5,4,3,2,1,0:T(8,128)} %bitcast.108, f32[4,2,2,2,80,512]{5,4,3,2,1,0:T(8,128)} %bitcast.110, ...), custom_call_target="tpu_custom_call" | custom-call | tf_op jit(solution)/shard_map/reduce_all/pallas_call | solution.py:928
  435.4 1.3 fusion.91
  436.6 1.4 multiply_reduce_fusion
  439.4 1.4 multiply_subtract_fusion
  442.4 1.7 convolution_bitcast_fusion.1
  444.8 1.5 fusion.41
  446.3 3.3 fusion.50
  449.7 2.2 fusion.35
  451.8 1.0 copy.117
  452.8 1.0 copy.118
  453.8 1.0 copy.119
  454.8 1.4 fusion.43
  456.2 2.3 fusion.20
  458.5 1.1 copy.114
  459.6 1.1 copy.115
  460.7 1.1 copy.116
  (85 shorter events, 12.3 us)
Async XLA Ops:
  0.7 441.8 %copy-start = (f32[448,448]{1,0:T(8,128)S(1)}, f32[448,448]{1,0:T(8,128)}, u32[]{:S(2)}) copy-start(f32[448,448]{1,0:T(8,128)} %param.35) | copy-start | bytes 2408452
  0.7 8.3 %copy-start.4 = (s32[4,1,128,192]{2,3,1,0:T(8,128)S(1)}, s32[4,1,128,192]{2,3,1,0:T(8,128)}, u32[]{:S(2)}) copy-start(s32[4,1,128,192]{2,3,1,0:T(8,128)} %param.26) | copy-start | bytes 1179652
  0.7 6.8 %copy-start.18 = (f32[256,32]{0,1:T(8,128)S(1)}, f32[256,32]{0,1:T(8,128)}, u32[]{:S(2)}) copy-start(f32[256,32]{0,1:T(8,128)} %param.32) | copy-start | bytes 98308
  0.7 7.7 %copy-start.19 = (f32[16,448]{1,0:T(8,128)S(1)}, f32[16,448]{1,0:T(8,128)}, u32[]{:S(2)}) copy-start(f32[16,448]{1,0:T(8,128)} %param.31) | copy-start | bytes 86020
  0.7 124.9 %copy-start.26 = (s32[4,1]{0,1:T(1,128)S(1)}, s32[4,1]{0,1:T(1,128)}, u32[]{:S(2)}) copy-start(s32[4,1]{0,1:T(1,128)} %param.28) | copy-start | bytes 52
  132.4 66.4 %copy-start.25 = (s32[4,2,1,128]{3,2,1,0:T(1,128)S(1)}, s32[4,2,1,128]{3,2,1,0:T(1,128)}, u32[]{:S(2)}) copy-start(s32[4,2,1,128]{3,2,1,0:T(1,128)} %get-tuple-element.70) | copy-start | bytes 12292
  132.4 68.0 %copy-start.5 = (bf16[4,2,128,384]{3,2,1,0:T(8,128)(2,1)S(1)}, bf16[4,2,128,384]{3,2,1,0:T(8,128)(2,1)}, u32[]{:S(2)}) copy-start(bf16[4,2,128,384]{3,2,1,0:T(8,128)(2,1)} %get-tuple-element.75) | copy-start | bytes 2359300
  201.2 67.7 %copy-start.24 = (f32[8,512]{1,0:T(8,128)S(1)}, f32[8,512]{1,0:T(8,128)}, u32[]{:S(2)}) copy-start(f32[8,512]{1,0:T(8,128)} %get-tuple-element.91) | copy-start | bytes 49156
  201.2 72.1 %copy-start.2 = (f32[512,128]{1,0:T(8,128)S(1)}, f32[512,128]{1,0:T(8,128)}, u32[]{:S(2)}) copy-start(f32[512,128]{1,0:T(8,128)} %get-tuple-element.88) | copy-start | bytes 786436
  201.2 72.4 %copy-start.7 = (f32[512,192]{1,0:T(8,128)S(1)}, f32[512,192]{1,0:T(8,128)}, u32[]{:S(2)}) copy-start(f32[512,192]{1,0:T(8,128)} %get-tuple-element.86) | copy-start | bytes 1179652
  271.6 4.5 copy-start.15
  276.0 163.4 %copy-start.12 = (f32[10,512]{1,0:T(8,128)S(1)}, f32[10,512]{1,0:T(8,128)}, u32[]{:S(2)}) copy-start(f32[10,512]{1,0:T(8,128)} %refs_4_.1) | copy-start | bytes 61444
  276.0 163.4 %copy-start.20 = (f32[10,512]{1,0:T(8,128)S(1)}, f32[10,512]{1,0:T(8,128)}, u32[]{:S(2)}) copy-start(f32[10,512]{1,0:T(8,128)} %param.45) | copy-start | bytes 61444
  276.0 163.4 %copy-start.21 = (f32[10,512]{1,0:T(8,128)S(1)}, f32[10,512]{1,0:T(8,128)}, u32[]{:S(2)}) copy-start(f32[10,512]{1,0:T(8,128)} %param.44) | copy-start | bytes 61444
  276.0 165.7 %copy-start.22 = (f32[256,32]{0,1:T(8,128)S(1)}, f32[256,32]{0,1:T(8,128)}, u32[]{:S(2)}) copy-start(f32[256,32]{0,1:T(8,128)} %param.43) | copy-start | bytes 98308
  276.1 165.7 %copy-start.23 = (f32[256,32]{0,1:T(8,128)S(1)}, f32[256,32]{0,1:T(8,128)}, u32[]{:S(2)}) copy-start(f32[256,32]{0,1:T(8,128)} %param.42) | copy-start | bytes 98308
  276.1 168.1 %copy-start.16 = (f32[16,448]{1,0:T(8,128)S(1)}, f32[16,448]{1,0:T(8,128)}, u32[]{:S(2)}) copy-start(f32[16,448]{1,0:T(8,128)} %param.40) | copy-start | bytes 86020
  276.1 168.1 %copy-start.17 = (f32[16,448]{1,0:T(8,128)S(1)}, f32[16,448]{1,0:T(8,128)}, u32[]{:S(2)}) copy-start(f32[16,448]{1,0:T(8,128)} %param.41) | copy-start | bytes 86020
  276.1 170.2 %copy-start.10 = (f32[80,2,512]{2,1,0:T(2,128)S(1)}, f32[80,2,512]{2,1,0:T(2,128)}, u32[]{:S(2)}) copy-start(f32[80,2,512]{2,1,0:T(2,128)} %param.39) | copy-start | bytes 983044
  276.1 170.2 %copy-start.11 = (f32[80,2,512]{2,1,0:T(2,128)S(1)}, f32[80,2,512]{2,1,0:T(2,128)}, u32[]{:S(2)}) copy-start(f32[80,2,512]{2,1,0:T(2,128)} %param.38) | copy-start | bytes 983044
  435.4 14.3 %copy-start.6 = (f32[80,2,512]{2,1,0:T(2,128)S(1)}, f32[80,2,512]{2,1,0:T(2,128)}, u32[]{:S(2)}) copy-start(f32[80,2,512]{2,1,0:T(2,128)} %param.30) | copy-start | bytes 983044
  441.8 7.8 %copy-start.1 = (f32[4,512,512]{2,1,0:T(8,128)S(1)}, f32[4,512,512]{2,1,0:T(8,128)}, u32[]{:S(2)}) copy-start(f32[4,512,512]{2,1,0:T(8,128)} %param.34) | copy-start | bytes 12582916
  446.3 8.5 %copy-start.8 = (f32[112,2,512]{2,1,0:T(2,128)S(1)}, f32[112,2,512]{2,1,0:T(2,128)}, u32[]{:S(2)}) copy-start(f32[112,2,512]{2,1,0:T(2,128)} %param.37) | copy-start | bytes 1376260
  446.3 8.5 %copy-start.9 = (f32[112,2,512]{2,1,0:T(2,128)S(1)}, f32[112,2,512]{2,1,0:T(2,128)}, u32[]{:S(2)}) copy-start(f32[112,2,512]{2,1,0:T(2,128)} %param.36) | copy-start | bytes 1376260
  446.3 8.5 %copy-start.13 = (f32[112,512]{1,0:T(8,128)S(1)}, f32[112,512]{1,0:T(8,128)}, u32[]{:S(2)}) copy-start(f32[112,512]{1,0:T(8,128)} %get-tuple-element.94) | copy-start | bytes 688132
  446.3 8.5 %copy-start.14 = (f32[112,512]{1,0:T(8,128)S(1)}, f32[112,512]{1,0:T(8,128)}, u32[]{:S(2)}) copy-start(f32[112,512]{1,0:T(8,128)} %get-tuple-element.93) | copy-start | bytes 688132
  449.6 6.5 %copy-start.3 = (f32[112,2,512]{2,1,0:T(2,128)S(1)}, f32[112,2,512]{2,1,0:T(2,128)}, u32[]{:S(2)}) copy-start(f32[112,2,512]{2,1,0:T(2,128)} %param.29) | copy-start | bytes 1376260
